TPU v7x, 256 devices: a whole 4x4x8 slice. The times are simulated.
256 devices in a mesh: blk: 128 (over z, y_hi, x, core), feat: 2 (over y_lo).
Axes of the slice: x: 4, y: 4 (y_hi: 2, y_lo: 2; y = y_hi * 2 + y_lo), z: 8, core: 2. Of those that a mesh axis runs over, the one named last changes fastest.
Arguments:
- features: bfloat16 [65536, 1024], P('blk', 'feat'), may hold values from -24 to 24
- weight_in: bfloat16 [1024, 1024], P(None, 'feat'), may hold values from -0.1875 to 0.1875
- weight_out: bfloat16 [1024, 1024], P(None, 'feat'), may hold values from -0.1875 to 0.1875
- adj_tiles: bfloat16 [128, 5, 8, 128, 128], P('blk'), may hold values from -0.625 to 0.625
- tile_rows: int32 [128, 5, 8], P('blk'), may hold values from 0 to 3, as said below
- tile_cols: int32 [128, 5, 8], P('blk'), may hold values from 0 to 3, as said below
- tile_counts: int32 [128, 5], P('blk'), may hold values from 0 to 8
- cotangent: bfloat16 [65536, 1024], P('blk', 'feat'), may hold values from -0.0625 to 0.0625
Outputs:
- layer_output: bfloat16 [65536, 1024], P('blk', 'feat')
- grad_weight_in: float32 [1024, 1024], P('blk', 'feat')
- grad_weight_out: float32 [1024, 1024], P('blk', 'feat')
Inputs may be any that keep to these rules, and one draw needn't show every extreme that they name: `tile_rows`: within one block and cycle step the 8 slots name distinct (row, column) tile pairs. `tile_cols`: within one block and cycle step the 8 slots name distinct (row, column) tile pairs.
All inputs are finite; a program needn't handle non-finite values.
Results may differ from a plain program's by a relative error of at most 0.0064.
Values may be sent and summed in bfloat16 or wider, within the bound.
A program may use at most 128 MiB of HBM per device.

v0:
```python
import jax
import jax.numpy as jnp
from jax import lax
from jax.sharding import PartitionSpec as P

RADIUS = 2


def from_behind(value, axis, steps):
    count = lax.axis_size(axis)
    pairs = [(source, (source + steps) % count) for source in range(count)]
    return lax.ppermute(value, axis, pairs)


def slot_weights(put_ids, live_count, block_rows):
    chosen = put_ids[:, None] == jnp.arange(block_rows, dtype=jnp.int32)[None, :]
    live_mask = (jnp.arange(put_ids.shape[0], dtype=jnp.int32) < live_count)[:, None]
    return (chosen & live_mask).astype(jnp.float32)


def step_terms(tile_set, row_ids, col_ids, live_count, source, flipped):
    block_rows = source.shape[0]
    if flipped:
        take_ids, put_ids = (row_ids, col_ids)
    else:
        take_ids, put_ids = (col_ids, row_ids)
    picked = jnp.take(source, take_ids, axis=0)
    pattern = "kba,kbw->kaw" if flipped else "kab,kbw->kaw"
    product = jnp.einsum(pattern, tile_set, picked, preferred_element_type=jnp.float32)
    weights = slot_weights(put_ids, live_count, block_rows)
    return jnp.einsum("kr,kaw->raw", weights, product, precision=lax.Precision.HIGHEST)


def blocked(values_in, tile_size):
    return values_in.reshape(values_in.shape[0] // tile_size, tile_size, values_in.shape[1])


def spread(values_in, adj_tiles, tile_rows, tile_cols, tile_counts):
    tile_size = adj_tiles.shape[-1]
    summed = step_terms(
        adj_tiles[0, RADIUS],
        tile_rows[0, RADIUS],
        tile_cols[0, RADIUS],
        tile_counts[0, RADIUS],
        blocked(values_in, tile_size),
        False,
    )
    for cycle_step in range(2 * RADIUS + 1):
        if cycle_step != RADIUS:
            neighbour = from_behind(values_in, "blk", RADIUS - cycle_step)
            summed = summed + step_terms(
                adj_tiles[0, cycle_step],
                tile_rows[0, cycle_step],
                tile_cols[0, cycle_step],
                tile_counts[0, cycle_step],
                blocked(neighbour, tile_size),
                False,
            )
    return summed.reshape(values_in.shape[0], values_in.shape[1])


def return_sum(values_in, adj_tiles, tile_rows, tile_cols, tile_counts):
    tile_size = adj_tiles.shape[-1]
    summed = step_terms(
        adj_tiles[0, RADIUS],
        tile_rows[0, RADIUS],
        tile_cols[0, RADIUS],
        tile_counts[0, RADIUS],
        blocked(values_in, tile_size),
        True,
    )
    for cycle_step in range(2 * RADIUS + 1):
        if cycle_step != RADIUS:
            offset = cycle_step - RADIUS
            partial_sum = step_terms(
                adj_tiles[0, cycle_step],
                tile_rows[0, cycle_step],
                tile_cols[0, cycle_step],
                tile_counts[0, cycle_step],
                blocked(values_in, tile_size),
                True,
            )
            arrived = from_behind(partial_sum, "blk", offset)
            summed = summed + arrived
    return summed.reshape(values_in.shape[0], values_in.shape[1])


def panels(values_in):
    return lax.all_gather(values_in, "feat", axis=1, tiled=True)


def shards(
    features, weight_in, weight_out, adj_tiles, tile_rows, tile_cols, tile_counts, cotangent
):
    spread_in = spread(features, adj_tiles, tile_rows, tile_cols, tile_counts).astype(jnp.bfloat16)
    full_in = panels(spread_in)
    pre_hidden = jnp.dot(full_in, weight_in, preferred_element_type=jnp.float32)
    hidden = jax.nn.silu(pre_hidden).astype(jnp.bfloat16)
    spread_hidden = spread(hidden, adj_tiles, tile_rows, tile_cols, tile_counts).astype(
        jnp.bfloat16
    )
    full_hidden = panels(spread_hidden)
    layer_output = jnp.dot(full_hidden, weight_out, preferred_element_type=jnp.float32).astype(
        jnp.bfloat16
    )
    partial_mix = lax.dot_general(
        cotangent, weight_out, (((1,), (1,)), ((), ())), preferred_element_type=jnp.float32
    )
    back_mixed = lax.psum_scatter(partial_mix, "feat", scatter_dimension=1, tiled=True).astype(
        jnp.bfloat16
    )
    back_hidden = return_sum(back_mixed, adj_tiles, tile_rows, tile_cols, tile_counts)
    sigmoid_gate = jax.nn.sigmoid(pre_hidden)
    back_pre = (back_hidden * sigmoid_gate * (1.0 + pre_hidden * (1.0 - sigmoid_gate))).astype(
        jnp.bfloat16
    )
    sliced = full_in
    grad_weight_in = lax.psum_scatter(
        lax.dot_general(
            sliced, back_pre, (((0,), (0,)), ((), ())), preferred_element_type=jnp.float32
        ),
        "blk",
        scatter_dimension=0,
        tiled=True,
    )
    sliced = full_hidden
    grad_weight_out = lax.psum_scatter(
        lax.dot_general(
            sliced, cotangent, (((0,), (0,)), ((), ())), preferred_element_type=jnp.float32
        ),
        "blk",
        scatter_dimension=0,
        tiled=True,
    )
    return (layer_output, grad_weight_in, grad_weight_out)


def solution(mesh):
    return jax.shard_map(
        shards,
        mesh=mesh,
        in_specs=(
            P("blk", "feat"),
            P(None, "feat"),
            P(None, "feat"),
            P("blk", None, None, None, None),
            P("blk", None, None),
            P("blk", None, None),
            P("blk", None),
            P("blk", "feat"),
        ),
        out_specs=(P("blk", "feat"), P("blk", "feat"), P("blk", "feat")),
        check_vma=False,
    )
```

profile of v0, /device:TPU:1, one launch (start us, length us, event | category | flops | bytes accessed | tf_op | source)
XLA Modules:
  0.0 1584.6 jit_solution(9753863811832958401)
XLA Ops:
  7.2 11.3 collective-permute-start.3
  20.3 3.2 fusion.225
  27.6 3.2 copy.15
  38.2 3.1 copy.19
  61.3 3.8 fusion.20
  72.0 3.2 fusion.76
  75.2 3.1 copy.28
  78.4 3.6 fusion.2
  83.9 3.2 fusion.80
  87.1 3.1 copy.26
  90.2 3.7 fusion.6
  93.9 7.4 collective-permute-start.8
  102.9 3.2 fusion.78
  106.0 3.1 copy.27
  109.2 3.6 fusion.4
  115.0 3.2 fusion.74
  118.1 3.1 copy.29
  121.3 3.8 fusion
  138.9 16.0 %collective-permute-done.11 = f32[4,128,512]{2,0,1:T(4,128)} collective-permute-done((f32[4,128,512]{2,0,1:T(4,128)}, f32[4,128,512]{2,0,1:T(4,128)}, u32[]{:S(2)}, u32[]{:S(2)}) %collective-permute-start.11) | collective-permute-done | bytes 1048608 | tf_op jit(solution)/shard_map/ppermute | solution.py:12
  154.9 4.2 fusion.63
  160.4 3.6 fusion.73
  165.7 8.0 collective-permute-start.7
  184.0 3.2 copy.23
  193.9 3.6 fusion.12
  201.1 3.2 copy.21
  204.3 3.8 fusion.14
  213.8 3.2 copy.24
  224.1 3.2 fusion.226
  227.4 19.6 %all-gather.5.cloned.1.call-done = bf16[512,1024]{1,0:T(8,128)(2,1)} async-done(((bf16[512,512]{1,0:T(8,128)(2,1)}), bf16[512,1024]{1,0:T(8,128)(2,1)}) %all-gather.5.cloned.1.call-update) | async-done | bytes 1048592 | tf_op jit(solution)/shard_map/all_gather | solution.py:89
  246.9 3.4 fusion.227
  251.8 660.1 %reduce-scatter.6.cloned.1.call-done = f32[8,512]{1,0:T(8,128)} async-done(((f32[1024,512]{1,0:T(8,128)}), f32[8,512]{1,0:T(8,128)}) %reduce-scatter.6.cloned.1.call-update) | async-done | bytes 16400 | tf_op jit(solution)/shard_map/reduce_scatter | solution.py:118
  911.9 665.8 %reduce-scatter.8.cloned.1.call-done = f32[8,512]{1,0:T(8,128)} async-done(((f32[1024,512]{1,0:T(8,128)}), f32[8,512]{1,0:T(8,128)}) %reduce-scatter.8.cloned.1.call-update) | async-done | bytes 16400 | tf_op jit(solution)/shard_map/reduce_scatter | solution.py:127
  (130 shorter events, 97.4 us)
Async XLA Ops:
  7.2 13.1 copy-start
  7.2 16.8 %copy-start.16 = (s32[1,5,8]{2,0,1:T(1,128)S(1)}, s32[1,5,8]{2,0,1:T(1,128)}, u32[]{:S(2)}) copy-start(s32[1,5,8]{2,0,1:T(1,128)} %param.15) | copy-start | bytes 484
  7.2 62.0 %reduce-scatter.4.cloned.1.call-start = ((), (), s32[]{:S(2)}) async-start(), calls=%async_computation.5 | async-start | bytes 3145728 | tf_op jit(solution)/shard_map/reduce_scatter | solution.py:109
  7.2 27.4 %collective-permute-start.3 = (bf16[512,512]{1,0:T(8,128)(2,1)}, bf16[512,512]{1,0:T(8,128)(2,1)}, u32[]{:S(2)}, u32[]{:S(2)}) collective-permute-start(bf16[512,512]{1,0:T(8,128)(2,1)} %param.10), channel_id=1, source_target_pairs={{0,252},{2,254},{4,0},{6,2},{8,4},{10,6},{12,8},{14,10},{16,12},{1... | collective-permute-start | bytes 1572872 | tf_op jit(solution)/shard_map/ppermute | solution.py:12
  18.5 22.8 %collective-permute-start.2 = (bf16[512,512]{1,0:T(8,128)(2,1)}, bf16[512,512]{1,0:T(8,128)(2,1)}, u32[]{:S(2)}, u32[]{:S(2)}) collective-permute-start(bf16[512,512]{1,0:T(8,128)(2,1)} %param.10), channel_id=1, source_target_pairs={{0,254},{2,0},{4,2},{6,4},{8,6},{10,8},{12,10},{14,12},{16,14},{18... | collective-permute-start | bytes 1572872 | tf_op jit(solution)/shard_map/ppermute | solution.py:12
  19.5 28.5 %collective-permute-start.1 = (bf16[512,512]{1,0:T(8,128)(2,1)}, bf16[512,512]{1,0:T(8,128)(2,1)}, u32[]{:S(2)}, u32[]{:S(2)}) collective-permute-start(bf16[512,512]{1,0:T(8,128)(2,1)} %param.10), channel_id=1, source_target_pairs={{0,2},{2,4},{4,6},{6,8},{8,10},{10,12},{12,14},{14,16},{16,18},{18... | collective-permute-start | bytes 1572872 | tf_op jit(solution)/shard_map/ppermute | solution.py:12
  20.3 34.4 %collective-permute-start = (bf16[512,512]{1,0:T(8,128)(2,1)}, bf16[512,512]{1,0:T(8,128)(2,1)}, u32[]{:S(2)}, u32[]{:S(2)}) collective-permute-start(bf16[512,512]{1,0:T(8,128)(2,1)} %param.10), channel_id=1, source_target_pairs={{0,4},{2,6},{4,8},{6,10},{8,12},{10,14},{12,16},{14,18},{16,20},{1... | collective-permute-start | bytes 1572872 | tf_op jit(solution)/shard_map/ppermute | solution.py:12
  23.4 2.3 copy-start.1
  23.5 136.9 %all-gather.3.cloned.1.call-start = ((), (), s32[]{:S(2)}) async-start(), calls=%async_computation.3 | async-start | bytes 1572864 | tf_op jit(solution)/shard_map/all_gather | solution.py:89
  27.6 3.2 copy-start.15
  27.6 6.3 copy-start.17
  61.3 3.8 copy-start.5
  65.0 2.1 copy-start.6
  82.0 56.9 %collective-permute-start.10 = (f32[4,128,512]{2,0,1:T(4,128)}, f32[4,128,512]{2,0,1:T(4,128)}, u32[]{:S(2)}, u32[]{:S(2)}) collective-permute-start(f32[4,128,512]{2,0,1:T(4,128)} %fusion.2), channel_id=1, source_target_pairs={{0,2},{2,4},{4,6},{6,8},{8,10},{10,12},{12,14},{14,16},{16,18},{18... | collective-permute-start | bytes 3145736 | tf_op jit(solution)/shard_map/ppermute | solution.py:12
  93.9 45.0 %collective-permute-start.8 = (f32[4,128,512]{2,0,1:T(4,128)}, f32[4,128,512]{2,0,1:T(4,128)}, u32[]{:S(2)}, u32[]{:S(2)}) collective-permute-start(f32[4,128,512]{2,0,1:T(4,128)} %fusion.6), channel_id=1, source_target_pairs={{0,252},{2,254},{4,0},{6,2},{8,4},{10,6},{12,8},{14,10},{16,12},{1... | collective-permute-start | bytes 3145736 | tf_op jit(solution)/shard_map/ppermute | solution.py:12
  112.8 26.1 %collective-permute-start.9 = (f32[4,128,512]{2,0,1:T(4,128)}, f32[4,128,512]{2,0,1:T(4,128)}, u32[]{:S(2)}, u32[]{:S(2)}) collective-permute-start(f32[4,128,512]{2,0,1:T(4,128)} %fusion.4), channel_id=1, source_target_pairs={{0,254},{2,0},{4,2},{6,4},{8,6},{10,8},{12,10},{14,12},{16,14},{18... | collective-permute-start | bytes 3145736 | tf_op jit(solution)/shard_map/ppermute | solution.py:12
  121.3 3.8 copy-start.3
  121.3 4.9 copy-start.9
  125.1 29.8 %collective-permute-start.11 = (f32[4,128,512]{2,0,1:T(4,128)}, f32[4,128,512]{2,0,1:T(4,128)}, u32[]{:S(2)}, u32[]{:S(2)}) collective-permute-start(f32[4,128,512]{2,0,1:T(4,128)} %fusion), channel_id=1, source_target_pairs={{0,4},{2,6},{4,8},{6,10},{8,12},{10,14},{12,16},{14,18},{16,20},{1... | collective-permute-start | bytes 3145736 | tf_op jit(solution)/shard_map/ppermute | solution.py:12
  130.7 116.2 %all-gather.5.cloned.1.call-start = ((), (), s32[]{:S(2)}) async-start(), calls=%async_computation.4 | async-start | bytes 1572864 | tf_op jit(solution)/shard_map/all_gather | solution.py:89
  164.0 16.4 %collective-permute-start.6 = (bf16[512,512]{1,0:T(8,128)(2,1)}, bf16[512,512]{1,0:T(8,128)(2,1)}, u32[]{:S(2)}, u32[]{:S(2)}) collective-permute-start(bf16[512,512]{1,0:T(8,128)(2,1)} %get-tuple-element.25), channel_id=1, source_target_pairs={{0,254},{2,0},{4,2},{6,4},{8,6},{10,8},{12,10},{14,12},{16,14},{18... | collective-permute-start | bytes 1572872 | tf_op jit(solution)/shard_map/ppermute | solution.py:12
  165.0 22.1 %collective-permute-start.5 = (bf16[512,512]{1,0:T(8,128)(2,1)}, bf16[512,512]{1,0:T(8,128)(2,1)}, u32[]{:S(2)}, u32[]{:S(2)}) collective-permute-start(bf16[512,512]{1,0:T(8,128)(2,1)} %get-tuple-element.25), channel_id=1, source_target_pairs={{0,2},{2,4},{4,6},{6,8},{8,10},{10,12},{12,14},{14,16},{16,18},{18... | collective-permute-start | bytes 1572872 | tf_op jit(solution)/shard_map/ppermute | solution.py:12
  165.7 31.8 %collective-permute-start.4 = (bf16[512,512]{1,0:T(8,128)(2,1)}, bf16[512,512]{1,0:T(8,128)(2,1)}, u32[]{:S(2)}, u32[]{:S(2)}) collective-permute-start(bf16[512,512]{1,0:T(8,128)(2,1)} %get-tuple-element.25), channel_id=1, source_target_pairs={{0,4},{2,6},{4,8},{6,10},{8,12},{10,14},{12,16},{14,18},{16,20},{1... | collective-permute-start | bytes 1572872 | tf_op jit(solution)/shard_map/ppermute | solution.py:12
  165.7 44.5 %collective-permute-start.7 = (bf16[512,512]{1,0:T(8,128)(2,1)}, bf16[512,512]{1,0:T(8,128)(2,1)}, u32[]{:S(2)}, u32[]{:S(2)}) collective-permute-start(bf16[512,512]{1,0:T(8,128)(2,1)} %get-tuple-element.25), channel_id=1, source_target_pairs={{0,252},{2,254},{4,0},{6,2},{8,4},{10,6},{12,8},{14,10},{16,12},{1... | collective-permute-start | bytes 1572872 | tf_op jit(solution)/shard_map/ppermute | solution.py:12
  204.3 3.8 copy-start.7
  213.8 6.1 copy-start.11
  217.0 2.8 copy-start.4
  217.0 2.8 copy-start.10
  223.6 688.3 %reduce-scatter.6.cloned.1.call-start = ((), (), s32[]{:S(2)}) async-start(), calls=%async_computation.6 | async-start | bytes 2113536 | tf_op jit(solution)/shard_map/reduce_scatter | solution.py:118
  224.1 22.8 %copy-start.12 = (bf16[512,512]{1,0:T(8,128)(2,1)S(1)}, bf16[512,512]{1,0:T(8,128)(2,1)}, u32[]{:S(2)}) copy-start(bf16[512,512]{1,0:T(8,128)(2,1)} %param.17) | copy-start | bytes 1572868
  227.3 1350.4 %reduce-scatter.8.cloned.1.call-start = ((), (), s32[]{:S(2)}) async-start(), calls=%async_computation.7 | async-start | bytes 2113536 | tf_op jit(solution)/shard_map/reduce_scatter | solution.py:127
  246.9 3.4 copy-start.14
  (3 other events, 4.9 us)
Sparse Core Ops, SparseCore 0:
  23.6 36.0 reduce-scatter.3
  130.9 29.5 all-gather.2
  223.7 23.1 all-gather.4
  249.8 662.0 reduce-scatter.5
  914.9 662.8 reduce-scatter.7
where the time goes:
time: 1600 us; the launch traced here: 1580 us
  waiting for transfers between devices  1360 us (85%)
  matrix products  95.7 us (6%)
  local copies, waits for them, and re-layouts  75.6 us (5%)
  starting transfers between devices  31.8 us (2%)
    reduce_scatter x1, waiting for transfers between devices, shards(): lax.psum_scatter(lax.dot_general(sliced, cotangent, (((0,), (0,)), ((), (...  666 us
    reduce_scatter x1, waiting for transfers between devices, shards(): lax.psum_scatter(lax.dot_general(sliced, back_pre, (((0,), (0,)), ((), ()...  660 us
    dot_general x15, local copies, waits for them, and re-layouts, step_terms(): jnp.einsum(pattern, tile_set, picked, preferred_element_type=jnp.float32)  47 us
    dot_general x15, matrix products, step_terms(): jnp.einsum('kr,kaw->raw', weights, product, precision=lax.Precision.HIGHEST)  46 us
    dot_general x15, matrix products, step_terms(): jnp.einsum(pattern, tile_set, picked, preferred_element_type=jnp.float32)  35 us
  transfers between devices with their start and end apart: 17, of which 5 were waited for; matrix products, arithmetic and copies ran while one was open for 9% of the time, Pallas kernels for 0%

commit v1 on v0

v1 whole, which is shorter than its diff:
```python
import functools

import jax
import jax.numpy as jnp
from jax import lax
from jax.experimental import pallas as pl
from jax.experimental.pallas import tpu as pltpu
from jax.sharding import PartitionSpec as P

F32 = jnp.float32
BF = jnp.bfloat16
MESH = pl.DeviceIdType.MESH
NB = 128
NZ, NY, NX, NC = 8, 2, 4, 2
N = 512
W = 512
TILE = 128
OFFS = (1, -1, 2, -2)
XCH = 2
XW = W // XCH
RCH = 2
RW = N // RCH
SUB = 256


def dot(a, b):
    return jnp.dot(a, b, preferred_element_type=F32)


def dot_tn(a, b):
    return lax.dot_general(a, b, (((0,), (0,)), ((), ())), preferred_element_type=F32)


def dot_nt(a, b):
    return lax.dot_general(a, b, (((1,), (1,)), ((), ())), preferred_element_type=F32)


def fold(v):
    return jnp.concatenate([v[..., : W // 2], v[..., W // 2 :]], axis=-2)


def loop(count, body):
    def step(i, carry):
        body(i)
        return carry

    lax.fori_loop(0, count, step, 0)


def span(i, size):
    return pl.ds(pl.multiple_of(i * size, size), size)


class Sems:
    def __init__(self, send, recv):
        self.send, self.recv, self.used = send, recv, 0

    def copy(self, src, dst, device):
        i = self.used
        self.used += 1
        made = pltpu.make_async_remote_copy(
            src_ref=src,
            dst_ref=dst,
            send_sem=self.send.at[i],
            recv_sem=self.recv.at[i],
            device_id=device,
            device_id_type=MESH,
        )
        made.start()
        return made


NREMOTE = 80


def kernel(
    x_h, win_h, wout_h, tiles_h, rows, cols, cnts, cot_h,
    out_o, gin_o, gout_o,
    x, win, wout, tiles, cot,
    a, xg, sacc, sfull, pre, hfull, dact, zacc, z, zg,
    pbuf, pr, cacc, cp, bhs, bhr, bp, oacc,
    g1, g1c, g1r1, g1x, g1r2f, g1r2, g1y, g1r3f, g1r3, g1z,
    g2, g2c, g2r1, g2z, g2r2f, g2r2, g2x, g2r3f, g2r3, g2y,
    lsem, ssem, rsem,
):
    b = lax.axis_index("blk")
    f = lax.axis_index("feat")
    c = lax.rem(b, NC)
    ix = lax.rem(b // NC, NX)
    iy = lax.rem(b // (NC * NX), NY)
    iz = b // (NC * NX * NY)
    nf = 1 - f
    nc = 1 - c

    def node(zz, yy, xx, cc):
        return (((zz * NY + yy) * NX + xx) * NC + cc, f)

    def near(o):
        return (lax.rem(b + o + NB, NB), f)

    peer = (b, nf)
    partner = node(iz, iy, ix, nc)
    xpeers = [lax.rem(ix + d, NX) for d in range(1, NX)]
    zpeers = [lax.rem(iz + d, NZ) for d in range(1, NZ)]
    ypeer = 1 - iy

    greeted = [near(o) for o in OFFS] + [peer, partner]
    greeted += [node(iz, iy, xx, c) for xx in xpeers]
    greeted += [node(zz, iy, ix, c) for zz in zpeers]
    greeted += [node(iz, ypeer, ix, c)]
    barrier = pltpu.get_barrier_semaphore()
    for device in greeted:
        pl.semaphore_signal(barrier, inc=1, device_id=device, device_id_type=MESH)
    loads = []
    for i, (src, dst) in enumerate(
        ((x_h, x), (tiles_h, tiles), (cot_h, cot), (win_h, win), (wout_h, wout))
    ):
        made = pltpu.make_async_copy(src, dst, lsem.at[i])
        made.start()
        loads.append(made)
    loads[0].wait()
    pl.semaphore_wait(barrier, len(greeted))

    sems = Sems(ssem, rsem)
    xcopies = []
    for j in range(XCH):
        cs = pl.ds(j * XW, XW)
        xcopies.append(
            [sems.copy(x.at[:, cs], xg.at[i, :, cs], near(-o)) for i, o in enumerate(OFFS)]
        )

    loads[1].wait()

    def densify(s):
        live = cnts[0, s]
        place = [
            jnp.where(k < live, rows[0, s, k] * 4 + cols[0, s, k], -1) for k in range(8)
        ]
        for r in range(4):
            for q in range(4):
                block = jnp.zeros((TILE, TILE), BF)
                for k in range(8):
                    block = lax.select(place[k] == r * 4 + q, tiles[s, k], block)
                a[s, r * TILE : (r + 1) * TILE, q * TILE : (q + 1) * TILE] = block

    loop(5, densify)
    loads[2].wait()

    def own_s(i):
        sacc[span(i, SUB), :] = dot(a[2, span(i, SUB), :], x[...])

    loop(N // SUB, own_s)

    pcopies = []
    for i, o in enumerate(OFFS):

        def product(k, i=i, o=o):
            pbuf[i, span(k, SUB), :] = dot_tn(a[o + 2, :, span(k, SUB)], cot[...]).astype(BF)

        loop(N // SUB, product)
        pcopies.append(sems.copy(pbuf.at[i], pr.at[i], near(o)))

    def own_c(k):
        cacc[span(k, SUB), :] = dot_tn(a[2, :, span(k, SUB)], cot[...])

    loop(N // SUB, own_c)

    scopies = []
    for j in range(XCH):
        cs = pl.ds(j * XW, XW)
        for i, o in enumerate(OFFS):
            xcopies[j][i].wait_recv()

            def add(k, i=i, o=o):
                rs = span(k, SUB)
                total = sacc[rs, cs] + dot(a[o + 2, rs, :], xg[i, :, cs])
                if i == len(OFFS) - 1:
                    sfull[f, rs, cs] = total.astype(BF)
                else:
                    sacc[rs, cs] = total

            loop(N // SUB, add)
        scopies.append(sems.copy(sfull.at[f, :, cs], sfull.at[f, :, cs], peer))

    loads[3].wait()

    def pre_own(k):
        rs = span(k, SUB)
        pre[rs, :] = dot(sfull[f, rs, :], win[f])

    loop(N // SUB, pre_own)
    for j in range(XCH - 1):
        cs = pl.ds(j * XW, XW)
        scopies[j].wait_recv()

        def pre_add(k):
            rs = span(k, SUB)
            pre[rs, :] += dot(sfull[nf, rs, cs], win[nf, cs, :])

        loop(N // SUB, pre_add)
    cs = pl.ds((XCH - 1) * XW, XW)
    scopies[-1].wait_recv()
    hcopies = []
    for j in range(RCH):

        def act(k, j=j):
            rs = pl.ds(pl.multiple_of(j * RW + k * TILE, TILE), TILE)
            v = pre[rs, :] + dot(sfull[nf, rs, cs], win[nf, cs, :])
            g = 1.0 / (1.0 + jnp.exp(-v))
            hfull[f, rs, :] = (v * g).astype(BF)
            dact[rs, :] = g * (1.0 + v * (1.0 - g))

        loop(RW // TILE, act)
        rs = pl.ds(j * RW, RW)
        hcopies.append(sems.copy(hfull.at[f, rs, :], hfull.at[f, rs, :], peer))

    loads[4].wait()

    def z_own(k):
        rs = span(k, SUB)
        zacc[rs, :] = dot(hfull[f, rs, :], wout[f])

    loop(N // SUB, z_own)
    zcopies = []
    for j in range(RCH):
        hcopies[j].wait_recv()
        rs = pl.ds(j * RW, RW)
        z[rs, :] = (zacc[rs, :] + dot(hfull[nf, rs, :], wout[nf])).astype(BF)
        zcopies.append(
            [sems.copy(z.at[rs, :], zg.at[i, rs, :], near(-o)) for i, o in enumerate(OFFS)]
        )

    for i in range(len(OFFS)):
        pcopies[i].wait_recv()

    def close_c(k):
        rs = span(k, TILE)
        total = cacc[rs, :]
        for i in range(len(OFFS)):
            total += pr[i, rs, :].astype(F32)
        cp[rs, :] = total.astype(BF)

    loop(N // TILE, close_c)

    def bh_other(k):
        rs = span(k, SUB)
        bhs[rs, :] = dot_nt(cp[rs, :], wout[nf]).astype(BF)

    loop(N // SUB, bh_other)
    bhcopy = sems.copy(bhs, bhr, peer)

    def gout_rows(k):
        part = dot_tn(hfull[k // 4, :, span(lax.rem(k, 4), TILE)], cp[...])
        g2[k] = part.reshape(NY, NX, NC, 8, W)

    loop(NZ, gout_rows)
    g2core = sems.copy(g2.at[:, :, :, nc], g2c, partner)

    def bh_own(k):
        rs = span(k, SUB)
        cacc[rs, :] = dot_nt(cp[rs, :], wout[f])

    loop(N // SUB, bh_own)

    g2core.wait_recv()

    def g2_first(k):
        g2r1[k] = fold(g2[k, :, :, c] + g2c[k]).astype(BF)

    loop(NZ, g2_first)
    g2zc = [
        sems.copy(g2r1.at[zz], g2z.at[d], node(zz, iy, ix, c)) for d, zz in enumerate(zpeers)
    ]

    bhcopy.wait_recv()

    def close_bp(k):
        rs = span(k, TILE)
        bp[rs, :] = ((cacc[rs, :] + bhr[rs, :].astype(F32)) * dact[rs, :]).astype(BF)

    loop(N // TILE, close_bp)

    def gin_rows(k):
        part = dot_tn(sfull[k // 4, :, span(lax.rem(k, 4), TILE)], bp[...])
        g1[k] = part.reshape(NY, NX, NC, 8, W)

    loop(NZ, gin_rows)
    g1core = sems.copy(g1.at[:, :, :, nc], g1c, partner)

    def own_o(k):
        rs = span(k, SUB)
        oacc[rs, :] = dot(a[2, rs, :], z[...])

    loop(N // SUB, own_o)

    g1core.wait_recv()

    def g1_first(k):
        g1r1[k] = fold(g1[k, :, :, c] + g1c[k]).astype(BF)

    loop(NZ, g1_first)
    g1xc = [
        sems.copy(g1r1.at[:, :, xx], g1x.at[d], node(iz, iy, xx, c))
        for d, xx in enumerate(xpeers)
    ]

    for j in range(RCH):
        ks = pl.ds(j * RW, RW)
        for i, o in enumerate(OFFS):
            zcopies[j][i].wait_recv()

            def out_add(k, i=i, o=o):
                rs = span(k, SUB)
                total = oacc[rs, :] + dot(a[o + 2, rs, ks], zg[i, ks, :])
                if i == len(OFFS) - 1 and j == RCH - 1:
                    out_o[rs, :] = total.astype(BF)
                else:
                    oacc[rs, :] = total

            loop(N // SUB, out_add)

    for copy in g2zc:
        copy.wait_recv()
    total = fold(g2[iz, :, :, c] + g2c[iz])
    for d in range(NZ - 1):
        total += g2z[d].astype(F32)
    g2r2f[...] = total
    g2r2[...] = total.astype(BF)
    g2xc = [
        sems.copy(g2r2.at[:, xx], g2x.at[d], node(iz, iy, xx, c)) for d, xx in enumerate(xpeers)
    ]

    for copy in g1xc:
        copy.wait_recv()

    def g1_second(k):
        total = fold(g1[k, :, ix, c] + g1c[k, :, ix])
        for d in range(NX - 1):
            total += g1x[d, k].astype(F32)
        g1r2f[k] = total
        g1r2[k] = total.astype(BF)

    loop(NZ, g1_second)
    g1yc = sems.copy(g1r2.at[:, ypeer], g1y, node(iz, ypeer, ix, c))

    for copy in g2xc:
        copy.wait_recv()
    total = g2r2f[:, ix]
    for d in range(NX - 1):
        total += g2x[d].astype(F32)
    g2r3f[...] = total
    g2r3[...] = total.astype(BF)
    g2yc = sems.copy(g2r3.at[ypeer], g2y, node(iz, ypeer, ix, c))

    g1yc.wait_recv()
    total = g1r2f[:, iy] + g1y[...].astype(F32)
    g1r3f[...] = total
    g1r3[...] = total.astype(BF)
    g1zc = [
        sems.copy(g1r3.at[zz], g1z.at[d], node(zz, iy, ix, c)) for d, zz in enumerate(zpeers)
    ]

    g2yc.wait_recv()
    total = g2r3f[iy] + g2y[...].astype(F32)
    gout_o[:, : W // 2] = total[:8]
    gout_o[:, W // 2 :] = total[8:]

    for copy in g1zc:
        copy.wait_recv()
    total = g1r3f[iz]
    for d in range(NZ - 1):
        total += g1z[d].astype(F32)
    gin_o[:, : W // 2] = total[:8]
    gin_o[:, W // 2 :] = total[8:]

    sent = [copy for group in xcopies + zcopies for copy in group] + pcopies + scopies + hcopies
    sent += [bhcopy, g2core, g1core, g1yc, g2yc] + g2zc + g1xc + g2xc + g1zc
    for copy in sent:
        copy.wait_send()


def shards(features, weight_in, weight_out, adj_tiles, tile_rows, tile_cols, tile_counts, cotangent):
    anyspace = pl.BlockSpec(memory_space=pl.ANY)
    smem = pl.BlockSpec(memory_space=pltpu.SMEM)
    vmem = pl.BlockSpec(memory_space=pltpu.VMEM)
    V = pltpu.VMEM
    scratch = [
        V((N, W), BF), V((2, 512, W), BF), V((2, 512, W), BF), V((5, 8, TILE, TILE), BF), V((N, W), BF),
        V((5, N, N), BF), V((4, N, W), BF), V((N, W), F32), V((2, N, W), BF), V((N, W), F32),
        V((2, N, W), BF), V((N, W), F32), V((N, W), F32), V((N, W), BF), V((4, N, W), BF),
        V((4, N, W), BF), V((4, N, W), BF), V((N, W), F32), V((N, W), BF), V((N, W), BF),
        V((N, W), BF), V((N, W), BF), V((N, W), F32),
        V((NZ, NY, NX, NC, 8, W), F32), V((NZ, NY, NX, 8, W), F32), V((NZ, NY, NX, 16, W // 2), BF),
        V((3, NZ, NY, 16, W // 2), BF), V((NZ, NY, 16, W // 2), F32), V((NZ, NY, 16, W // 2), BF),
        V((NZ, 16, W // 2), BF), V((NZ, 16, W // 2), F32), V((NZ, 16, W // 2), BF),
        V((7, 16, W // 2), BF),
        V((NZ, NY, NX, NC, 8, W), F32), V((NZ, NY, NX, 8, W), F32), V((NZ, NY, NX, 16, W // 2), BF),
        V((7, NY, NX, 16, W // 2), BF), V((NY, NX, 16, W // 2), F32), V((NY, NX, 16, W // 2), BF),
        V((3, NY, 16, W // 2), BF), V((NY, 16, W // 2), F32), V((NY, 16, W // 2), BF),
        V((16, W // 2), BF),
        pltpu.SemaphoreType.DMA((5,)),
        pltpu.SemaphoreType.DMA((NREMOTE,)),
        pltpu.SemaphoreType.DMA((NREMOTE,)),
    ]
    return pl.pallas_call(
        kernel,
        out_shape=(
            jax.ShapeDtypeStruct((N, W), BF),
            jax.ShapeDtypeStruct((8, W), F32),
            jax.ShapeDtypeStruct((8, W), F32),
        ),
        in_specs=[anyspace, anyspace, anyspace, anyspace, smem, smem, smem, anyspace],
        out_specs=(vmem, vmem, vmem),
        scratch_shapes=scratch,
        compiler_params=pltpu.CompilerParams(
            collective_id=0, has_side_effects=True, vmem_limit_bytes=60 * 1024 * 1024
        ),
        name="graph_layers",
    )(
        features,
        weight_in.reshape(2, 512, W),
        weight_out.reshape(2, 512, W),
        adj_tiles.reshape(5, 8, TILE, TILE),
        tile_rows,
        tile_cols,
        tile_counts,
        cotangent,
    )


def solution(mesh):
    return jax.shard_map(
        shards,
        mesh=mesh,
        in_specs=(
            P("blk", "feat"),
            P(None, "feat"),
            P(None, "feat"),
            P("blk", None, None, None, None),
            P("blk", None, None),
            P("blk", None, None),
            P("blk", None),
            P("blk", "feat"),
        ),
        out_specs=(P("blk", "feat"), P("blk", "feat"), P("blk", "feat")),
        check_vma=False,
    )
```

time: 1600 us -> 133 us (0.08)
  waiting for transfers between devices: 1360 us -> 0 us
  Pallas kernels: 0 us -> 123 us
  matrix products: 95.7 us -> 0 us
  local copies, waits for them, and re-layouts: 75.6 us -> 7.07 us
  starting transfers between devices: 31.8 us -> 0 us
    reduce_scatter x3 -> x0, waiting for transfers between devices: 1330 us -> none  [the longest x1 666 us: shards(): lax.psum_scatter(lax.dot_general(sliced, cotangent, (((0,), (0,)), ((), (...]
    pallas_call x0 -> x1, Pallas kernels: none -> 123 us  [shards(): pl.pallas_call(kernel, out_shape=(jax.ShapeDtypeStruct((N, W), BF), jax.S...]
    dot_general x35 -> x0, matrix products: 95.7 us -> none  [the longest x15 46 us: step_terms(): jnp.einsum('kr,kaw->raw', weights, product, precision=lax.Precision.HIGHEST)]
    dot_general x15 -> x0, local copies, waits for them, and re-layouts: 47 us -> none  [step_terms(): jnp.einsum(pattern, tile_set, picked, preferred_element_type=jnp.float32)]
    ppermute x12 -> x0, starting transfers between devices: 30.9 us -> none  [from_behind(): return lax.ppermute(value, axis, pairs)]
    gather x15 -> x0, local copies, waits for them, and re-layouts: 24.6 us -> none  [step_terms(): picked = jnp.take(source, take_ids, axis=0)]
    all_gather x2 -> x0, waiting for transfers between devices: 20.5 us -> none  [panels(): return lax.all_gather(values_in, 'feat', axis=1, tiled=True)]
    ppermute x12 -> x0, waiting for transfers between devices: 16 us -> none  [from_behind(): return lax.ppermute(value, axis, pairs)]
  transfers between devices with their start and end apart: 17 -> 0, of which waited for: 5 -> 0; matrix products, arithmetic and copies ran while one was open for 9% -> 0% of each run, Pallas kernels for 0% -> 0%
where the time goes in v1:
time: 133 us; the launch traced here: 131 us
  Pallas kernels  123 us (92%)
  local copies, waits for them, and re-layouts  7.07 us (5%)
    pallas_call x1, Pallas kernels, shards(): pl.pallas_call(kernel, out_shape=(jax.ShapeDtypeStruct((N, W), BF), jax.S...  123 us
    unnamed x5, local copies, waits for them, and re-layouts  7.07 us

profile of v1, /device:TPU:1, one launch (start us, length us, event | category | flops | bytes accessed | tf_op | source)
XLA Modules:
  0.0 130.7 jit_solution(18327400792794883437)
XLA Ops:
  0.6 1.3 copy.11.rows
  1.9 1.3 copy.12.cols
  3.2 123.0 %graph_layers.1 = (bf16[512,512]{1,0:T(8,128)(2,1)}, f32[8,512]{1,0:T(8,128)}, f32[8,512]{1,0:T(8,128)}) custom-call(bf16[512,512]{1,0:T(8,128)(2,1)} %x_h.1, bf16[2,512,512]{2,1,0:T(8,128)(2,1)} %bitcast.4, bf16[2,512,512]{2,1,0:T(8,128)(2,1)} %bitcast.5, bf16[5,8,128,128]{3,2,1,0:T(8,128)(2,1)} %bitcast.3, s32[1,5,8]{2,1,0:T(8,128)} %copy.11.rows, ...), custom_call_target="tpu_custom_call" | custom-call | tf_op jit(solution)/shard_map/graph_layers/pallas_call | solution.py:405
  126.2 1.9 %copy.16 = bf16[512,512]{1,0:T(8,128)(2,1)} copy(bf16[512,512]{1,0:T(8,128)(2,1)} %get-tuple-element.6) | data formatting | bytes 1048576
  128.0 1.3 %copy.17 = f32[8,512]{1,0:T(8,128)} copy(f32[8,512]{1,0:T(8,128)} %get-tuple-element.7) | data formatting | bytes 32768
  129.4 1.3 %copy.18 = f32[8,512]{1,0:T(8,128)} copy(f32[8,512]{1,0:T(8,128)} %get-tuple-element.8) | data formatting | bytes 32768

commit v2 on v1

--- a/solution.py
+++ b/solution.py
@@ -15,10 +15,10 @@
 N = 512
 W = 512
 TILE = 128
-OFFS = (1, -1, 2, -2)
 XCH = 2
 XW = W // XCH
 RCH = 2
+PWHEN = 0
 RW = N // RCH
 SUB = 256
 
@@ -104,7 +104,7 @@
     zpeers = [lax.rem(iz + d, NZ) for d in range(1, NZ)]
     ypeer = 1 - iy
 
-    greeted = [near(o) for o in OFFS] + [peer, partner]
+    greeted = [near(2), near(-2), peer, partner]
     greeted += [node(iz, iy, xx, c) for xx in xpeers]
     greeted += [node(zz, iy, ix, c) for zz in zpeers]
     greeted += [node(iz, ypeer, ix, c)]
@@ -122,19 +122,35 @@
     pl.semaphore_wait(barrier, len(greeted))
 
     sems = Sems(ssem, rsem)
+    step_of = (0, 4, 3 - 2 * c, 1 + 2 * c)
+
+    def spread(src, dst):
+        return [
+            sems.copy(src, dst(0), near(2)),
+            sems.copy(src, dst(1), near(-2)),
+            sems.copy(src, dst(2), partner),
+        ]
+
+    def on_side(copies, side):
+        @pl.when(side == 0)
+        def _():
+            copies[0].wait_recv()
+
+        @pl.when(side == 1)
+        def _():
+            copies[1].wait_recv()
+
     xcopies = []
     for j in range(XCH):
         cs = pl.ds(j * XW, XW)
-        xcopies.append(
-            [sems.copy(x.at[:, cs], xg.at[i, :, cs], near(-o)) for i, o in enumerate(OFFS)]
-        )
+        xcopies.append(spread(x.at[:, cs], lambda i, cs=cs: xg.at[i, :, cs]))
 
     loads[1].wait()
 
     def densify(s):
         live = cnts[0, s]
         place = [
-            jnp.where(k < live, rows[0, s, k] * 4 + cols[0, s, k], -1) for k in range(8)
+            jnp.where(k < live, rows[s, 0, k] * 4 + cols[s, 0, k], -1) for k in range(8)
         ]
         for r in range(4):
             for q in range(4):
@@ -151,36 +167,65 @@
 
     loop(N // SUB, own_s)
 
-    pcopies = []
-    for i, o in enumerate(OFFS):
-
-        def product(k, i=i, o=o):
-            pbuf[i, span(k, SUB), :] = dot_tn(a[o + 2, :, span(k, SUB)], cot[...]).astype(BF)
-
-        loop(N // SUB, product)
-        pcopies.append(sems.copy(pbuf.at[i], pr.at[i], near(o)))
+
+    def product(slot, step, helped):
+        def rows_of(k):
+            rs = span(k, SUB)
+            part = dot_tn(a[step, :, rs], cot[...])
+            if helped:
+                part += pr[3, rs, :].astype(F32)
+            pbuf[slot, rs, :] = part.astype(BF)
+
+        loop(N // SUB, rows_of)
+
+    product(2, step_of[2], False)
+    pcopies = [sems.copy(pbuf.at[2], pr.at[2], partner)]
+    product(3, step_of[3], False)
+    help_copy = sems.copy(pbuf.at[3], pr.at[3], partner)
+    product(c, 4 * c, False)
 
     def own_c(k):
         cacc[span(k, SUB), :] = dot_tn(a[2, :, span(k, SUB)], cot[...])
 
     loop(N // SUB, own_c)
-
+    help_copy.wait_recv()
+    product(nc, 4 * nc, True)
+
+    def send_products():
+        pcopies.append(sems.copy(pbuf.at[c], pr.at[c], near(4 * c - 2)))
+        pcopies.append(sems.copy(pbuf.at[nc], pr.at[nc], near(4 * nc - 2)))
+
+    if PWHEN == 0:
+        send_products()
     scopies = []
+    relays = []
     for j in range(XCH):
         cs = pl.ds(j * XW, XW)
-        for i, o in enumerate(OFFS):
-            xcopies[j][i].wait_recv()
-
-            def add(k, i=i, o=o):
+
+        def add(i, last=False):
+            def rows_of(k):
                 rs = span(k, SUB)
-                total = sacc[rs, cs] + dot(a[o + 2, rs, :], xg[i, :, cs])
-                if i == len(OFFS) - 1:
+                total = sacc[rs, cs] + dot(a[step_of[i], rs, :], xg[i, :, cs])
+                if last:
                     sfull[f, rs, cs] = total.astype(BF)
                 else:
                     sacc[rs, cs] = total
 
-            loop(N // SUB, add)
+            loop(N // SUB, rows_of)
+
+        xcopies[j][2].wait_recv()
+        add(2)
+        on_side(xcopies[j], nc)
+        relay = sems.copy(xg.at[nc, :, cs], xg.at[3, :, cs], partner)
+        relays.append(relay)
+        on_side(xcopies[j], c)
+        add(0)
+        add(1)
+        relay.wait_recv()
+        add(3, True)
         scopies.append(sems.copy(sfull.at[f, :, cs], sfull.at[f, :, cs], peer))
+    if PWHEN == 1:
+        send_products()
 
     loads[3].wait()
 
@@ -200,6 +245,8 @@
         loop(N // SUB, pre_add)
     cs = pl.ds((XCH - 1) * XW, XW)
     scopies[-1].wait_recv()
+    if PWHEN == 2:
+        send_products()
     hcopies = []
     for j in range(RCH):
 
@@ -226,17 +273,15 @@
         hcopies[j].wait_recv()
         rs = pl.ds(j * RW, RW)
         z[rs, :] = (zacc[rs, :] + dot(hfull[nf, rs, :], wout[nf])).astype(BF)
-        zcopies.append(
-            [sems.copy(z.at[rs, :], zg.at[i, rs, :], near(-o)) for i, o in enumerate(OFFS)]
-        )
-
-    for i in range(len(OFFS)):
-        pcopies[i].wait_recv()
+        zcopies.append(spread(z.at[rs, :], lambda i, rs=rs: zg.at[i, rs, :]))
+
+    for copy in pcopies:
+        copy.wait_recv()
 
     def close_c(k):
         rs = span(k, TILE)
         total = cacc[rs, :]
-        for i in range(len(OFFS)):
+        for i in range(3):
             total += pr[i, rs, :].astype(F32)
         cp[rs, :] = total.astype(BF)
 
@@ -306,18 +351,27 @@
 
     for j in range(RCH):
         ks = pl.ds(j * RW, RW)
-        for i, o in enumerate(OFFS):
-            zcopies[j][i].wait_recv()
-
-            def out_add(k, i=i, o=o):
-                rs = span(k, SUB)
-                total = oacc[rs, :] + dot(a[o + 2, rs, ks], zg[i, ks, :])
-                if i == len(OFFS) - 1 and j == RCH - 1:
-                    out_o[rs, :] = total.astype(BF)
-                else:
-                    oacc[rs, :] = total
-
-            loop(N // SUB, out_add)
+        on_side(zcopies[j], nc)
+        relays.append(sems.copy(zg.at[nc, ks, :], zg.at[3, ks, :], partner))
+        zcopies[j][2].wait_recv()
+        on_side(zcopies[j], c)
+
+    def out_add(k):
+        rs = span(k, SUB)
+        total = oacc[rs, :]
+        for i in range(3):
+            total += dot(a[step_of[i], rs, :], zg[i])
+        oacc[rs, :] = total
+
+    loop(N // SUB, out_add)
+    for relay in relays[XCH:]:
+        relay.wait_recv()
+
+    def out_last(k):
+        rs = span(k, SUB)
+        out_o[rs, :] = (oacc[rs, :] + dot(a[step_of[3], rs, :], zg[3])).astype(BF)
+
+    loop(N // SUB, out_last)
 
     for copy in g2zc:
         copy.wait_recv()
@@ -373,10 +427,16 @@
     gin_o[:, : W // 2] = total[:8]
     gin_o[:, W // 2 :] = total[8:]
 
-    sent = [copy for group in xcopies + zcopies for copy in group] + pcopies + scopies + hcopies
-    sent += [bhcopy, g2core, g1core, g1yc, g2yc] + g2zc + g1xc + g2xc + g1zc
+    sent = [copy for group in xcopies + zcopies for copy in group] + pcopies + scopies + hcopies + relays
+    sent += [help_copy, bhcopy, g2core, g1core, g1yc, g2yc] + g2zc + g1xc + g2xc + g1zc
     for copy in sent:
         copy.wait_send()
+
+
+def hand_over(a_ref, b_ref, c_ref, a_o, b_o, c_o):
+    a_o[...] = a_ref[...]
+    b_o[...] = b_ref[...]
+    c_o[...] = c_ref[...]
 
 
 def shards(features, weight_in, weight_out, adj_tiles, tile_rows, tile_cols, tile_counts, cotangent):
@@ -402,7 +462,7 @@
         pltpu.SemaphoreType.DMA((NREMOTE,)),
         pltpu.SemaphoreType.DMA((NREMOTE,)),
     ]
-    return pl.pallas_call(
+    results = pl.pallas_call(
         kernel,
         out_shape=(
             jax.ShapeDtypeStruct((N, W), BF),
@@ -421,11 +481,18 @@
         weight_in.reshape(2, 512, W),
         weight_out.reshape(2, 512, W),
         adj_tiles.reshape(5, 8, TILE, TILE),
-        tile_rows,
-        tile_cols,
+        tile_rows.transpose(1, 0, 2),
+        tile_cols.transpose(1, 0, 2),
         tile_counts,
         cotangent,
     )
+    return pl.pallas_call(
+        hand_over,
+        out_shape=tuple(jax.ShapeDtypeStruct(r.shape, r.dtype) for r in results),
+        in_specs=[vmem] * 3,
+        out_specs=[vmem] * 3,
+        name="hand_over",
+    )(*results)
 
 
 def solution(mesh):

time: 133 us -> 112 us (0.84)
  the two profiles are of different devices: /device:TPU:1 before, /device:TPU:4 now
where the time goes in v2:
time: 112 us
  Pallas kernels  112 us (100%)
    pallas_call x1, Pallas kernels, shards(): pl.pallas_call(kernel, out_shape=(jax.ShapeDtypeStruct((N, W), BF), jax.S...  110 us

profile of v2, /device:TPU:4, one launch (start us, length us, event | category | flops | bytes accessed | tf_op | source)
XLA Modules:
  0.0 112.2 jit_solution(16841825835900820419)
XLA Ops:
  0.6 109.6 %graph_layers.1 = (bf16[512,512]{1,0:T(8,128)(2,1)}, f32[8,512]{1,0:T(8,128)}, f32[8,512]{1,0:T(8,128)}) custom-call(bf16[512,512]{1,0:T(8,128)(2,1)} %x_h.1, bf16[2,512,512]{2,1,0:T(8,128)(2,1)} %bitcast.6, bf16[2,512,512]{2,1,0:T(8,128)(2,1)} %bitcast.7, bf16[5,8,128,128]{3,2,1,0:T(8,128)(2,1)} %bitcast.5, s32[5,1,8]{2,1,0:T(1,128)} %bitcast.8, ...), custom_call_target="tpu_custom_call" | custom-call | tf_op jit(solution)/shard_map/graph_layers/pallas_call | solution.py:465
  110.3 1.9 %hand_over.1 = (bf16[512,512]{1,0:T(8,128)(2,1)}, f32[8,512]{1,0:T(8,128)}, f32[8,512]{1,0:T(8,128)}) custom-call(bf16[512,512]{1,0:T(8,128)(2,1)} %get-tuple-element.6.a_ref, f32[8,512]{1,0:T(8,128)} %get-tuple-element.7.b_ref, f32[8,512]{1,0:T(8,128)} %get-tuple-element.8.c_ref), custom_call_target="tpu_custom_call" | custom-call | tf_op jit(solution)/shard_map/hand_over/pallas_call | solution.py:489

commit v3 on v2

--- a/solution.py
+++ b/solution.py
@@ -55,10 +55,10 @@
     def __init__(self, send, recv):
         self.send, self.recv, self.used = send, recv, 0
 
-    def copy(self, src, dst, device):
+    def make(self, src, dst, device):
         i = self.used
         self.used += 1
-        made = pltpu.make_async_remote_copy(
+        return pltpu.make_async_remote_copy(
             src_ref=src,
             dst_ref=dst,
             send_sem=self.send.at[i],
@@ -66,8 +66,45 @@
             device_id=device,
             device_id_type=MESH,
         )
+
+    def copy(self, src, dst, device):
+        made = self.make(src, dst, device)
         made.start()
         return made
+
+
+class Swap:
+    def __init__(self, sems, edge, lo, hi, way, peer, turn, onward):
+        self.edge = edge
+        self.lo = sems.copy(lo[0], lo[1], peer)
+        self.straight = sems.make(hi[0], hi[1], peer)
+        self.out = sems.make(hi[0], way, turn)
+        self.on = sems.make(way, hi[2], onward)
+        self.pick(self.out.start, self.straight.start)
+
+    def pick(self, at_edge, inside):
+        pl.when(self.edge)(lambda: at_edge())
+        pl.when(jnp.logical_not(self.edge))(lambda: inside())
+
+    def pass_on(self):
+        @pl.when(jnp.logical_not(self.edge))
+        def _():
+            self.out.wait_recv()
+            self.on.start()
+
+    def wait_recv(self):
+        self.pass_on()
+        self.lo.wait_recv()
+        self.pick(self.on.wait_recv, self.straight.wait_recv)
+
+    def wait_send(self):
+        self.lo.wait_send()
+
+        def inside():
+            self.straight.wait_send()
+            self.on.wait_send()
+
+        self.pick(self.out.wait_send, inside)
 
 
 NREMOTE = 80
@@ -78,8 +115,8 @@
     out_o, gin_o, gout_o,
     x, win, wout, tiles, cot,
     a, xg, sacc, sfull, pre, hfull, dact, zacc, z, zg,
-    pbuf, pr, cacc, cp, bhs, bhr, bp, oacc,
-    g1, g1c, g1r1, g1x, g1r2f, g1r2, g1y, g1r3f, g1r3, g1z,
+    pbuf, pr, cacc, cfull, wq, bp, oacc, sway,
+    g1, g1c, g1r1, g1x, g1r2f, g1r2, g1y, g1r3, g1z,
     g2, g2c, g2r1, g2z, g2r2f, g2r2, g2x, g2r3f, g2r3, g2y,
     lsem, ssem, rsem,
 ):
@@ -99,18 +136,39 @@
         return (lax.rem(b + o + NB, NB), f)
 
     peer = (b, nf)
+    edge = jnp.logical_or(ix == 0, ix == NX - 1)
+    beside = ix + 1 - 2 * lax.rem(ix, 2)
+    beside_node = (((iz * NY + iy) * NX + beside) * NC + c)
+    turn, onward = (beside_node, nf), (beside_node, f)
     partner = node(iz, iy, ix, nc)
     xpeers = [lax.rem(ix + d, NX) for d in range(1, NX)]
     zpeers = [lax.rem(iz + d, NZ) for d in range(1, NZ)]
     ypeer = 1 - iy
 
-    greeted = [near(2), near(-2), peer, partner]
+    greeted = [near(2), near(-2), peer, partner, turn]
     greeted += [node(iz, iy, xx, c) for xx in xpeers]
     greeted += [node(zz, iy, ix, c) for zz in zpeers]
     greeted += [node(iz, ypeer, ix, c)]
+
+    def owner(zz):
+        return (((f * 4 + lax.rem(zz, 4)) * NY + iy) * NX + ix) * NC + c, zz // 4
+
+    def giver(zz):
+        return ((zz * NY + iy) * NX + ix) * NC + c, iz // 4
+
+    at_home = iz // 4 == f
+    mine = f * 4 + lax.rem(iz, 4)
+    greeted += [owner(zz) for zz in zpeers]
+    greeted += [giver(lax.rem(mine + d, NZ)) for d in range(1, NZ)]
     barrier = pltpu.get_barrier_semaphore()
     for device in greeted:
         pl.semaphore_signal(barrier, inc=1, device_id=device, device_id_type=MESH)
+
+    @pl.when(jnp.logical_not(at_home))
+    def _():
+        pl.semaphore_signal(barrier, inc=1, device_id=owner(iz), device_id_type=MESH)
+        pl.semaphore_signal(barrier, inc=1, device_id=giver(mine), device_id_type=MESH)
+
     loads = []
     for i, (src, dst) in enumerate(
         ((x_h, x), (tiles_h, tiles), (cot_h, cot), (win_h, win), (wout_h, wout))
@@ -119,10 +177,20 @@
         made.start()
         loads.append(made)
     loads[0].wait()
-    pl.semaphore_wait(barrier, len(greeted))
+    pl.semaphore_wait(barrier, len(greeted) + 2 * lax.rem(iz // 4 + f, 2))
 
     sems = Sems(ssem, rsem)
     step_of = (0, 4, 3 - 2 * c, 1 + 2 * c)
+
+    def swap(ref, out_slot, in_slot, start, size, cs, way):
+        half = size // 2
+        lo, hi = pl.ds(start, half), pl.ds(start + half, half)
+        return Swap(
+            sems, edge,
+            (ref(out_slot, lo, cs), ref(in_slot[0], lo, cs)),
+            (ref(out_slot, hi, cs), ref(in_slot[0], hi, cs), ref(in_slot[1], hi, cs)),
+            way, peer, turn, onward,
+        )
 
     def spread(src, dst):
         return [
@@ -161,6 +229,9 @@
 
     loop(5, densify)
     loads[2].wait()
+    loads[4].wait()
+    half = pl.ds(pl.multiple_of(c * (N // 2), N // 2), N // 2)
+    wqcopy = sems.copy(wout.at[nf, half, :], wq.at[half, :], peer)
 
     def own_s(i):
         sacc[span(i, SUB), :] = dot(a[2, span(i, SUB), :], x[...])
@@ -223,10 +294,14 @@
         add(1)
         relay.wait_recv()
         add(3, True)
-        scopies.append(sems.copy(sfull.at[f, :, cs], sfull.at[f, :, cs], peer))
+        scopies.append(
+            swap(lambda i, r, q: sfull.at[i, r, q], f, (f, nf), 0, N, cs, sway.at[:, cs])
+        )
     if PWHEN == 1:
         send_products()
 
+    wqcopy.wait_recv()
+    wqpass = sems.copy(wq.at[half, :], wq.at[half, :], partner)
     loads[3].wait()
 
     def pre_own(k):
@@ -247,6 +322,20 @@
     scopies[-1].wait_recv()
     if PWHEN == 2:
         send_products()
+    for copy in pcopies:
+        copy.wait_recv()
+
+    def close_c(k):
+        rs = span(k, TILE)
+        total = cacc[rs, :]
+        for i in range(3):
+            total += pr[i, rs, :].astype(F32)
+        cfull[f, rs, :] = total.astype(BF)
+
+    loop(N // TILE, close_c)
+
+    ccopy = sems.copy(cfull.at[f], cfull.at[f], peer)
+
     hcopies = []
     for j in range(RCH):
 
@@ -261,13 +350,65 @@
         rs = pl.ds(j * RW, RW)
         hcopies.append(sems.copy(hfull.at[f, rs, :], hfull.at[f, rs, :], peer))
 
-    loads[4].wait()
-
     def z_own(k):
         rs = span(k, SUB)
         zacc[rs, :] = dot(hfull[f, rs, :], wout[f])
 
     loop(N // SUB, z_own)
+    def bh_own(k):
+        rs = span(k, SUB)
+        cacc[rs, :] = dot_nt(cfull[f, rs, :], wout[f])
+
+    loop(N // SUB, bh_own)
+
+    def gout_cols(side):
+        def rows_of(k):
+            part = dot_tn(hfull[f, :, span(k, TILE)], cfull[side])
+            g1[side * 4 + k] = part.reshape(NY, NX, NC, 8, W)
+
+        loop(4, rows_of)
+
+    gout_cols(f)
+    ccopy.wait_recv()
+    wqpass.wait_recv()
+
+    def close_bp(k):
+        rs = span(k, TILE)
+        back = cacc[rs, :] + dot_nt(cfull[nf, rs, :], wq[...])
+        bp[rs, :] = (back * dact[rs, :]).astype(BF)
+
+    loop(N // TILE, close_bp)
+
+    def gin_rows(k):
+        part = dot_tn(sfull[k // 4, :, span(lax.rem(k, 4), TILE)], bp[...])
+        g2[k] = part.reshape(NY, NX, NC, 8, W)
+
+    loop(NZ, gin_rows)
+    g2core = sems.copy(g2.at[:, :, :, nc], g2c, partner)
+    gout_cols(nf)
+    g1core = sems.copy(g1.at[:, :, :, nc], g1c, partner)
+
+    g2core.wait_recv()
+
+    def g2_first(k):
+        g2r1[k] = fold(g2[k, :, :, c] + g2c[k]).astype(BF)
+
+    loop(NZ, g2_first)
+    g2zc = [
+        sems.copy(g2r1.at[zz], g2z.at[d], node(zz, iy, ix, c)) for d, zz in enumerate(zpeers)
+    ]
+
+    g1core.wait_recv()
+
+    def g1_first(k):
+        g1r1[k] = fold(g1[k, :, :, c] + g1c[k]).astype(BF)
+
+    loop(NZ, g1_first)
+    g1xc = [
+        sems.copy(g1r1.at[:, :, xx], g1x.at[d], node(iz, iy, xx, c))
+        for d, xx in enumerate(xpeers)
+    ]
+
     zcopies = []
     for j in range(RCH):
         hcopies[j].wait_recv()
@@ -275,103 +416,11 @@
         z[rs, :] = (zacc[rs, :] + dot(hfull[nf, rs, :], wout[nf])).astype(BF)
         zcopies.append(spread(z.at[rs, :], lambda i, rs=rs: zg.at[i, rs, :]))
 
-    for copy in pcopies:
-        copy.wait_recv()
-
-    def close_c(k):
-        rs = span(k, TILE)
-        total = cacc[rs, :]
-        for i in range(3):
-            total += pr[i, rs, :].astype(F32)
-        cp[rs, :] = total.astype(BF)
-
-    loop(N // TILE, close_c)
-
-    def bh_other(k):
-        rs = span(k, SUB)
-        bhs[rs, :] = dot_nt(cp[rs, :], wout[nf]).astype(BF)
-
-    loop(N // SUB, bh_other)
-    bhcopy = sems.copy(bhs, bhr, peer)
-
-    def gout_rows(k):
-        part = dot_tn(hfull[k // 4, :, span(lax.rem(k, 4), TILE)], cp[...])
-        g2[k] = part.reshape(NY, NX, NC, 8, W)
-
-    loop(NZ, gout_rows)
-    g2core = sems.copy(g2.at[:, :, :, nc], g2c, partner)
-
-    def bh_own(k):
-        rs = span(k, SUB)
-        cacc[rs, :] = dot_nt(cp[rs, :], wout[f])
-
-    loop(N // SUB, bh_own)
-
-    g2core.wait_recv()
-
-    def g2_first(k):
-        g2r1[k] = fold(g2[k, :, :, c] + g2c[k]).astype(BF)
-
-    loop(NZ, g2_first)
-    g2zc = [
-        sems.copy(g2r1.at[zz], g2z.at[d], node(zz, iy, ix, c)) for d, zz in enumerate(zpeers)
-    ]
-
-    bhcopy.wait_recv()
-
-    def close_bp(k):
-        rs = span(k, TILE)
-        bp[rs, :] = ((cacc[rs, :] + bhr[rs, :].astype(F32)) * dact[rs, :]).astype(BF)
-
-    loop(N // TILE, close_bp)
-
-    def gin_rows(k):
-        part = dot_tn(sfull[k // 4, :, span(lax.rem(k, 4), TILE)], bp[...])
-        g1[k] = part.reshape(NY, NX, NC, 8, W)
-
-    loop(NZ, gin_rows)
-    g1core = sems.copy(g1.at[:, :, :, nc], g1c, partner)
-
     def own_o(k):
         rs = span(k, SUB)
         oacc[rs, :] = dot(a[2, rs, :], z[...])
 
     loop(N // SUB, own_o)
-
-    g1core.wait_recv()
-
-    def g1_first(k):
-        g1r1[k] = fold(g1[k, :, :, c] + g1c[k]).astype(BF)
-
-    loop(NZ, g1_first)
-    g1xc = [
-        sems.copy(g1r1.at[:, :, xx], g1x.at[d], node(iz, iy, xx, c))
-        for d, xx in enumerate(xpeers)
-    ]
-
-    for j in range(RCH):
-        ks = pl.ds(j * RW, RW)
-        on_side(zcopies[j], nc)
-        relays.append(sems.copy(zg.at[nc, ks, :], zg.at[3, ks, :], partner))
-        zcopies[j][2].wait_recv()
-        on_side(zcopies[j], c)
-
-    def out_add(k):
-        rs = span(k, SUB)
-        total = oacc[rs, :]
-        for i in range(3):
-            total += dot(a[step_of[i], rs, :], zg[i])
-        oacc[rs, :] = total
-
-    loop(N // SUB, out_add)
-    for relay in relays[XCH:]:
-        relay.wait_recv()
-
-    def out_last(k):
-        rs = span(k, SUB)
-        out_o[rs, :] = (oacc[rs, :] + dot(a[step_of[3], rs, :], zg[3])).astype(BF)
-
-    loop(N // SUB, out_last)
 
     for copy in g2zc:
         copy.wait_recv()
@@ -384,6 +433,13 @@
         sems.copy(g2r2.at[:, xx], g2x.at[d], node(iz, iy, xx, c)) for d, xx in enumerate(xpeers)
     ]
 
+    for j in range(RCH):
+        ks = pl.ds(j * RW, RW)
+        on_side(zcopies[j], nc)
+        relays.append(sems.copy(zg.at[nc, ks, :], zg.at[3, ks, :], partner))
+        zcopies[j][2].wait_recv()
+        on_side(zcopies[j], c)
+
     for copy in g1xc:
         copy.wait_recv()
 
@@ -406,31 +462,56 @@
     g2r3[...] = total.astype(BF)
     g2yc = sems.copy(g2r3.at[ypeer], g2y, node(iz, ypeer, ix, c))
 
+    def out_add(k):
+        rs = span(k, SUB)
+        total = oacc[rs, :]
+        for i in range(3):
+            total += dot(a[step_of[i], rs, :], zg[i])
+        oacc[rs, :] = total
+
+    loop(N // SUB, out_add)
+    for relay in relays[XCH:]:
+        relay.wait_recv()
+
+    def out_last(k):
+        rs = span(k, SUB)
+        out_o[rs, :] = (oacc[rs, :] + dot(a[step_of[3], rs, :], zg[3])).astype(BF)
+
+    loop(N // SUB, out_last)
+
     g1yc.wait_recv()
     total = g1r2f[:, iy] + g1y[...].astype(F32)
-    g1r3f[...] = total
     g1r3[...] = total.astype(BF)
     g1zc = [
-        sems.copy(g1r3.at[zz], g1z.at[d], node(zz, iy, ix, c)) for d, zz in enumerate(zpeers)
+        sems.copy(g1r3.at[zz], g1z.at[d + 1], owner(zz)) for d, zz in enumerate(zpeers)
     ]
+    g1last = sems.make(g1r3.at[iz], g1z.at[0], owner(iz))
+
+    @pl.when(at_home)
+    def _():
+        g1z[0] = g1r3[iz]
+
+    pl.when(jnp.logical_not(at_home))(lambda: g1last.start())
 
     g2yc.wait_recv()
     total = g2r3f[iy] + g2y[...].astype(F32)
+    gin_o[:, : W // 2] = total[:8]
+    gin_o[:, W // 2 :] = total[8:]
+
+    for copy in g1zc:
+        copy.wait_recv()
+    pl.when(jnp.logical_not(at_home))(lambda: g1last.wait_recv())
+    total = g1z[0].astype(F32)
+    for d in range(1, NZ):
+        total += g1z[d].astype(F32)
     gout_o[:, : W // 2] = total[:8]
     gout_o[:, W // 2 :] = total[8:]
 
-    for copy in g1zc:
-        copy.wait_recv()
-    total = g1r3f[iz]
-    for d in range(NZ - 1):
-        total += g1z[d].astype(F32)
-    gin_o[:, : W // 2] = total[:8]
-    gin_o[:, W // 2 :] = total[8:]
-
     sent = [copy for group in xcopies + zcopies for copy in group] + pcopies + scopies + hcopies + relays
-    sent += [help_copy, bhcopy, g2core, g1core, g1yc, g2yc] + g2zc + g1xc + g2xc + g1zc
+    sent += [help_copy, wqcopy, wqpass, ccopy, g2core, g1core, g1yc, g2yc] + g2zc + g1xc + g2xc + g1zc
     for copy in sent:
         copy.wait_send()
+    pl.when(jnp.logical_not(at_home))(lambda: g1last.wait_send())
 
 
 def hand_over(a_ref, b_ref, c_ref, a_o, b_o, c_o):
@@ -448,12 +529,12 @@
         V((N, W), BF), V((2, 512, W), BF), V((2, 512, W), BF), V((5, 8, TILE, TILE), BF), V((N, W), BF),
         V((5, N, N), BF), V((4, N, W), BF), V((N, W), F32), V((2, N, W), BF), V((N, W), F32),
         V((2, N, W), BF), V((N, W), F32), V((N, W), F32), V((N, W), BF), V((4, N, W), BF),
-        V((4, N, W), BF), V((4, N, W), BF), V((N, W), F32), V((N, W), BF), V((N, W), BF),
-        V((N, W), BF), V((N, W), BF), V((N, W), F32),
+        V((4, N, W), BF), V((4, N, W), BF), V((N, W), F32), V((2, N, W), BF), V((N, W), BF),
+        V((N, W), BF), V((N, W), F32), V((N // 2, W), BF),
         V((NZ, NY, NX, NC, 8, W), F32), V((NZ, NY, NX, 8, W), F32), V((NZ, NY, NX, 16, W // 2), BF),
         V((3, NZ, NY, 16, W // 2), BF), V((NZ, NY, 16, W // 2), F32), V((NZ, NY, 16, W // 2), BF),
-        V((NZ, 16, W // 2), BF), V((NZ, 16, W // 2), F32), V((NZ, 16, W // 2), BF),
-        V((7, 16, W // 2), BF),
+        V((NZ, 16, W // 2), BF), V((NZ, 16, W // 2), BF),
+        V((NZ, 16, W // 2), BF),
         V((NZ, NY, NX, NC, 8, W), F32), V((NZ, NY, NX, 8, W), F32), V((NZ, NY, NX, 16, W // 2), BF),
         V((7, NY, NX, 16, W // 2), BF), V((NY, NX, 16, W // 2), F32), V((NY, NX, 16, W // 2), BF),
         V((3, NY, 16, W // 2), BF), V((NY, 16, W // 2), F32), V((NY, 16, W // 2), BF),

time: 112 us -> 105 us (0.938)
  the two profiles are of different devices: /device:TPU:4 before, /device:TPU:1 now
where the time goes in v3:
time: 105 us; the launch traced here: 104 us
  Pallas kernels  103 us (98%)
    pallas_call x1, Pallas kernels, shards(): pl.pallas_call(kernel, out_shape=(jax.ShapeDtypeStruct((N, W), BF), jax.S...  102 us

profile of v3, /device:TPU:1, one launch (start us, length us, event | category | flops | bytes accessed | tf_op | source)
XLA Modules:
  0.0 104.1 jit_solution(17646953407345999703)
XLA Ops:
  0.6 101.5 %graph_layers.1 = (bf16[512,512]{1,0:T(8,128)(2,1)}, f32[8,512]{1,0:T(8,128)}, f32[8,512]{1,0:T(8,128)}) custom-call(bf16[512,512]{1,0:T(8,128)(2,1)} %x_h.1, bf16[2,512,512]{2,1,0:T(8,128)(2,1)} %bitcast.6, bf16[2,512,512]{2,1,0:T(8,128)(2,1)} %bitcast.7, bf16[5,8,128,128]{3,2,1,0:T(8,128)(2,1)} %bitcast.5, s32[5,1,8]{2,1,0:T(1,128)} %bitcast.8, ...), custom_call_target="tpu_custom_call" | custom-call | tf_op jit(solution)/shard_map/graph_layers/pallas_call | solution.py:546
  102.2 1.9 %hand_over.1 = (bf16[512,512]{1,0:T(8,128)(2,1)}, f32[8,512]{1,0:T(8,128)}, f32[8,512]{1,0:T(8,128)}) custom-call(bf16[512,512]{1,0:T(8,128)(2,1)} %get-tuple-element.6.a_ref, f32[8,512]{1,0:T(8,128)} %get-tuple-element.7.b_ref, f32[8,512]{1,0:T(8,128)} %get-tuple-element.8.c_ref), custom_call_target="tpu_custom_call" | custom-call | tf_op jit(solution)/shard_map/hand_over/pallas_call | solution.py:570

commit v4 on v3

--- a/solution.py
+++ b/solution.py
@@ -17,8 +17,9 @@
 TILE = 128
 XCH = 2
 XW = W // XCH
-RCH = 2
+RCH = 4
 PWHEN = 0
+SPLIT = 3
 RW = N // RCH
 SUB = 256
 
@@ -107,12 +108,13 @@
         self.pick(self.out.wait_send, inside)
 
 
-NREMOTE = 80
+NREMOTE = 112
 
 
 def kernel(
-    x_h, win_h, wout_h, tiles_h, rows, cols, cnts, cot_h,
-    out_o, gin_o, gout_o,
+    x_h, win_h, wout_h, tiles_h, rows_h, cols_h, cnts_h, cot_h,
+    out_h, gin_h, gout_h,
+    rows, cols, cnts, out_o, gin_o, gout_o,
     x, win, wout, tiles, cot,
     a, xg, sacc, sfull, pre, hfull, dact, zacc, z, zg,
     pbuf, pr, cacc, cfull, wq, bp, oacc, sway,
@@ -140,12 +142,13 @@
     beside = ix + 1 - 2 * lax.rem(ix, 2)
     beside_node = (((iz * NY + iy) * NX + beside) * NC + c)
     turn, onward = (beside_node, nf), (beside_node, f)
+    across = (((iz * NY + 1 - iy) * NX + ix) * NC + c, nf)
     partner = node(iz, iy, ix, nc)
     xpeers = [lax.rem(ix + d, NX) for d in range(1, NX)]
     zpeers = [lax.rem(iz + d, NZ) for d in range(1, NZ)]
     ypeer = 1 - iy
 
-    greeted = [near(2), near(-2), peer, partner, turn]
+    greeted = [near(2), near(-2), peer, partner, turn, across]
     greeted += [node(iz, iy, xx, c) for xx in xpeers]
     greeted += [node(zz, iy, ix, c) for zz in zpeers]
     greeted += [node(iz, ypeer, ix, c)]
@@ -171,7 +174,8 @@
 
     loads = []
     for i, (src, dst) in enumerate(
-        ((x_h, x), (tiles_h, tiles), (cot_h, cot), (win_h, win), (wout_h, wout))
+        ((x_h, x), (tiles_h, tiles), (cot_h, cot), (win_h, win), (wout_h, wout),
+         (rows_h, rows), (cols_h, cols), (cnts_h, cnts))
     ):
         made = pltpu.make_async_copy(src, dst, lsem.at[i])
         made.start()
@@ -183,8 +187,8 @@
     step_of = (0, 4, 3 - 2 * c, 1 + 2 * c)
 
     def swap(ref, out_slot, in_slot, start, size, cs, way):
-        half = size // 2
-        lo, hi = pl.ds(start, half), pl.ds(start + half, half)
+        near_rows = size * SPLIT // 4
+        lo, hi = pl.ds(start, near_rows), pl.ds(start + near_rows, size - near_rows)
         return Swap(
             sems, edge,
             (ref(out_slot, lo, cs), ref(in_slot[0], lo, cs)),
@@ -213,7 +217,8 @@
         cs = pl.ds(j * XW, XW)
         xcopies.append(spread(x.at[:, cs], lambda i, cs=cs: xg.at[i, :, cs]))
 
-    loads[1].wait()
+    for i in (1, 5, 6, 7):
+        loads[i].wait()
 
     def densify(s):
         live = cnts[0, s]
@@ -231,7 +236,7 @@
     loads[2].wait()
     loads[4].wait()
     half = pl.ds(pl.multiple_of(c * (N // 2), N // 2), N // 2)
-    wqcopy = sems.copy(wout.at[nf, half, :], wq.at[half, :], peer)
+    wqcopy = sems.copy(wout.at[nf, half, :], wq.at[half, :], across)
 
     def own_s(i):
         sacc[span(i, SUB), :] = dot(a[2, span(i, SUB), :], x[...])
@@ -422,6 +427,19 @@
 
     loop(N // SUB, own_o)
 
+    for copy in g1xc:
+        copy.wait_recv()
+
+    def g1_second(k):
+        total = fold(g1[k, :, ix, c] + g1c[k, :, ix])
+        for d in range(NX - 1):
+            total += g1x[d, k].astype(F32)
+        g1r2f[k] = total
+        g1r2[k] = total.astype(BF)
+
+    loop(NZ, g1_second)
+    g1yc = sems.copy(g1r2.at[:, ypeer], g1y, node(iz, ypeer, ix, c))
+
     for copy in g2zc:
         copy.wait_recv()
     total = fold(g2[iz, :, :, c] + g2c[iz])
@@ -433,25 +451,19 @@
         sems.copy(g2r2.at[:, xx], g2x.at[d], node(iz, iy, xx, c)) for d, xx in enumerate(xpeers)
     ]
 
-    for j in range(RCH):
-        ks = pl.ds(j * RW, RW)
-        on_side(zcopies[j], nc)
-        relays.append(sems.copy(zg.at[nc, ks, :], zg.at[3, ks, :], partner))
-        zcopies[j][2].wait_recv()
-        on_side(zcopies[j], c)
-
-    for copy in g1xc:
-        copy.wait_recv()
-
-    def g1_second(k):
-        total = fold(g1[k, :, ix, c] + g1c[k, :, ix])
-        for d in range(NX - 1):
-            total += g1x[d, k].astype(F32)
-        g1r2f[k] = total
-        g1r2[k] = total.astype(BF)
-
-    loop(NZ, g1_second)
-    g1yc = sems.copy(g1r2.at[:, ypeer], g1y, node(iz, ypeer, ix, c))
+    g1yc.wait_recv()
+    total = g1r2f[:, iy] + g1y[...].astype(F32)
+    g1r3[...] = total.astype(BF)
+    g1zc = [
+        sems.copy(g1r3.at[zz], g1z.at[d + 1], owner(zz)) for d, zz in enumerate(zpeers)
+    ]
+    g1last = sems.make(g1r3.at[iz], g1z.at[0], owner(iz))
+
+    @pl.when(at_home)
+    def _():
+        g1z[0] = g1r3[iz]
+
+    pl.when(jnp.logical_not(at_home))(lambda: g1last.start())
 
     for copy in g2xc:
         copy.wait_recv()
@@ -462,6 +474,13 @@
     g2r3[...] = total.astype(BF)
     g2yc = sems.copy(g2r3.at[ypeer], g2y, node(iz, ypeer, ix, c))
 
+    for j in range(RCH):
+        ks = pl.ds(j * RW, RW)
+        on_side(zcopies[j], nc)
+        relays.append(sems.copy(zg.at[nc, ks, :], zg.at[3, ks, :], partner))
+        zcopies[j][2].wait_recv()
+        on_side(zcopies[j], c)
+
     def out_add(k):
         rs = span(k, SUB)
         total = oacc[rs, :]
@@ -473,30 +492,19 @@
     for relay in relays[XCH:]:
         relay.wait_recv()
 
-    def out_last(k):
-        rs = span(k, SUB)
+    stores = []
+    for k in range(N // SUB):
+        rs = pl.ds(k * SUB, SUB)
         out_o[rs, :] = (oacc[rs, :] + dot(a[step_of[3], rs, :], zg[3])).astype(BF)
-
-    loop(N // SUB, out_last)
-
-    g1yc.wait_recv()
-    total = g1r2f[:, iy] + g1y[...].astype(F32)
-    g1r3[...] = total.astype(BF)
-    g1zc = [
-        sems.copy(g1r3.at[zz], g1z.at[d + 1], owner(zz)) for d, zz in enumerate(zpeers)
-    ]
-    g1last = sems.make(g1r3.at[iz], g1z.at[0], owner(iz))
-
-    @pl.when(at_home)
-    def _():
-        g1z[0] = g1r3[iz]
-
-    pl.when(jnp.logical_not(at_home))(lambda: g1last.start())
+        stores.append(pltpu.make_async_copy(out_o.at[rs, :], out_h.at[rs, :], lsem.at[10 + k]))
+        stores[-1].start()
 
     g2yc.wait_recv()
     total = g2r3f[iy] + g2y[...].astype(F32)
     gin_o[:, : W // 2] = total[:8]
     gin_o[:, W // 2 :] = total[8:]
+    stores.append(pltpu.make_async_copy(gin_o, gin_h, lsem.at[8]))
+    stores[-1].start()
 
     for copy in g1zc:
         copy.wait_recv()
@@ -506,31 +514,45 @@
         total += g1z[d].astype(F32)
     gout_o[:, : W // 2] = total[:8]
     gout_o[:, W // 2 :] = total[8:]
+    stores.append(pltpu.make_async_copy(gout_o, gout_h, lsem.at[9]))
+    stores[-1].start()
 
     sent = [copy for group in xcopies + zcopies for copy in group] + pcopies + scopies + hcopies + relays
     sent += [help_copy, wqcopy, wqpass, ccopy, g2core, g1core, g1yc, g2yc] + g2zc + g1xc + g2xc + g1zc
+    for copy in stores:
+        copy.wait()
     for copy in sent:
         copy.wait_send()
     pl.when(jnp.logical_not(at_home))(lambda: g1last.wait_send())
 
 
-def hand_over(a_ref, b_ref, c_ref, a_o, b_o, c_o):
-    a_o[...] = a_ref[...]
-    b_o[...] = b_ref[...]
-    c_o[...] = c_ref[...]
+def hand_over(a_ref, b_ref, c_ref, a_o, b_o, c_o, a_v, b_v, c_v, insem, outsem):
+    moves = [(b_ref, b_v, b_o), (c_ref, c_v, c_o)]
+    for k in range(4):
+        rs = pl.ds(k * (N // 4), N // 4)
+        moves.append((a_ref.at[rs, :], a_v.at[rs, :], a_o.at[rs, :]))
+    taken = [pltpu.make_async_copy(m[0], m[1], insem.at[i]) for i, m in enumerate(moves)]
+    given = [pltpu.make_async_copy(m[1], m[2], outsem.at[i]) for i, m in enumerate(moves)]
+    for copy in taken:
+        copy.start()
+    for into, out in zip(taken, given):
+        into.wait()
+        out.start()
+    for copy in given:
+        copy.wait()
 
 
 def shards(features, weight_in, weight_out, adj_tiles, tile_rows, tile_cols, tile_counts, cotangent):
     anyspace = pl.BlockSpec(memory_space=pl.ANY)
-    smem = pl.BlockSpec(memory_space=pltpu.SMEM)
-    vmem = pl.BlockSpec(memory_space=pltpu.VMEM)
     V = pltpu.VMEM
     scratch = [
+        pltpu.SMEM((5, 1, 8), jnp.int32), pltpu.SMEM((5, 1, 8), jnp.int32), pltpu.SMEM((1, 5), jnp.int32),
+        V((N, W), BF), V((8, W), F32), V((8, W), F32),
         V((N, W), BF), V((2, 512, W), BF), V((2, 512, W), BF), V((5, 8, TILE, TILE), BF), V((N, W), BF),
         V((5, N, N), BF), V((4, N, W), BF), V((N, W), F32), V((2, N, W), BF), V((N, W), F32),
         V((2, N, W), BF), V((N, W), F32), V((N, W), F32), V((N, W), BF), V((4, N, W), BF),
         V((4, N, W), BF), V((4, N, W), BF), V((N, W), F32), V((2, N, W), BF), V((N, W), BF),
-        V((N, W), BF), V((N, W), F32), V((N // 2, W), BF),
+        V((N, W), BF), V((N, W), F32), V((N - N * SPLIT // 4, W), BF),
         V((NZ, NY, NX, NC, 8, W), F32), V((NZ, NY, NX, 8, W), F32), V((NZ, NY, NX, 16, W // 2), BF),
         V((3, NZ, NY, 16, W // 2), BF), V((NZ, NY, 16, W // 2), F32), V((NZ, NY, 16, W // 2), BF),
         V((NZ, 16, W // 2), BF), V((NZ, 16, W // 2), BF),
@@ -539,7 +561,7 @@
         V((7, NY, NX, 16, W // 2), BF), V((NY, NX, 16, W // 2), F32), V((NY, NX, 16, W // 2), BF),
         V((3, NY, 16, W // 2), BF), V((NY, 16, W // 2), F32), V((NY, 16, W // 2), BF),
         V((16, W // 2), BF),
-        pltpu.SemaphoreType.DMA((5,)),
+        pltpu.SemaphoreType.DMA((8 + 2 + N // SUB,)),
         pltpu.SemaphoreType.DMA((NREMOTE,)),
         pltpu.SemaphoreType.DMA((NREMOTE,)),
     ]
@@ -550,8 +572,8 @@
             jax.ShapeDtypeStruct((8, W), F32),
             jax.ShapeDtypeStruct((8, W), F32),
         ),
-        in_specs=[anyspace, anyspace, anyspace, anyspace, smem, smem, smem, anyspace],
-        out_specs=(vmem, vmem, vmem),
+        in_specs=[anyspace] * 8,
+        out_specs=(anyspace,) * 3,
         scratch_shapes=scratch,
         compiler_params=pltpu.CompilerParams(
             collective_id=0, has_side_effects=True, vmem_limit_bytes=60 * 1024 * 1024
@@ -570,8 +592,12 @@
     return pl.pallas_call(
         hand_over,
         out_shape=tuple(jax.ShapeDtypeStruct(r.shape, r.dtype) for r in results),
-        in_specs=[vmem] * 3,
-        out_specs=[vmem] * 3,
+        in_specs=[anyspace] * 3,
+        out_specs=[anyspace] * 3,
+        scratch_shapes=[
+            V((N, W), BF), V((8, W), F32), V((8, W), F32),
+            pltpu.SemaphoreType.DMA((6,)), pltpu.SemaphoreType.DMA((6,)),
+        ],
         name="hand_over",
     )(*results)
 

time: 105 us -> 99.5 us (0.948)
  Pallas kernels: 103 us -> 98.7 us
    pallas_call x1, Pallas kernels: 102 us -> 96.8 us  [shards(): pl.pallas_call(kernel, out_shape=(jax.ShapeDtypeStruct((N, W), BF), jax.S...]
where the time goes in v4:
time: 99.5 us; the launch traced here: 99.3 us
  Pallas kernels  98.7 us (99%)
    pallas_call x1, Pallas kernels, shards(): pl.pallas_call(kernel, out_shape=(jax.ShapeDtypeStruct((N, W), BF), jax.S...  96.8 us

profile of v4, /device:TPU:1, one launch (start us, length us, event | category | flops | bytes accessed | tf_op | source)
XLA Modules:
  0.0 99.3 jit_solution(5946209120476974620)
XLA Ops:
  0.6 96.8 %graph_layers.1 = (bf16[512,512]{1,0:T(8,128)(2,1)}, f32[8,512]{1,0:T(8,128)}, f32[8,512]{1,0:T(8,128)}) custom-call(bf16[512,512]{1,0:T(8,128)(2,1)} %x_h.1, bf16[2,512,512]{2,1,0:T(8,128)(2,1)} %bitcast.6, bf16[2,512,512]{2,1,0:T(8,128)(2,1)} %bitcast.7, bf16[5,8,128,128]{3,2,1,0:T(8,128)(2,1)} %bitcast.5, s32[5,1,8]{2,1,0:T(1,128)} %bitcast.8, ...), custom_call_target="tpu_custom_call" | custom-call | tf_op jit(solution)/shard_map/graph_layers/pallas_call | solution.py:568
  97.5 1.9 %hand_over.1 = (bf16[512,512]{1,0:T(8,128)(2,1)}, f32[8,512]{1,0:T(8,128)}, f32[8,512]{1,0:T(8,128)}) custom-call(bf16[512,512]{1,0:T(8,128)(2,1)} %get-tuple-element.6.a_ref, f32[8,512]{1,0:T(8,128)} %get-tuple-element.7.b_ref, f32[8,512]{1,0:T(8,128)} %get-tuple-element.8.c_ref), custom_call_target="tpu_custom_call" | custom-call | tf_op jit(solution)/shard_map/hand_over/pallas_call | solution.py:592

commit v5 on v4

--- a/solution.py
+++ b/solution.py
@@ -68,6 +68,14 @@
             device_id_type=MESH,
         )
 
+    def choose(self, first, src, other, dst, device, other_device):
+        made = self.make(src, dst, device)
+        self.used -= 1
+        turned = self.make(other, dst, other_device)
+        pl.when(first)(lambda: made.start())
+        pl.when(jnp.logical_not(first))(lambda: turned.start())
+        return made
+
     def copy(self, src, dst, device):
         made = self.make(src, dst, device)
         made.start()
@@ -116,10 +124,10 @@
     out_h, gin_h, gout_h,
     rows, cols, cnts, out_o, gin_o, gout_o,
     x, win, wout, tiles, cot,
-    a, xg, sacc, sfull, pre, hfull, dact, zacc, z, zg,
+    a, xg, sacc, sfull, pre, hfull, dact, zacc, z, z2, zg,
     pbuf, pr, cacc, cfull, wq, bp, oacc, sway,
-    g1, g1c, g1r1, g1x, g1r2f, g1r2, g1y, g1r3, g1z,
-    g2, g2c, g2r1, g2z, g2r2f, g2r2, g2x, g2r3f, g2r3, g2y,
+    g1, g1c, g1r1, g1x, g1r2f, g1r2, g1l,
+    g2, g2c, g2r1, g2x, g2r2f, g2r2, g2l,
     lsem, ssem, rsem,
 ):
     b = lax.axis_index("blk")
@@ -151,26 +159,21 @@
     greeted = [near(2), near(-2), peer, partner, turn, across]
     greeted += [node(iz, iy, xx, c) for xx in xpeers]
     greeted += [node(zz, iy, ix, c) for zz in zpeers]
-    greeted += [node(iz, ypeer, ix, c)]
-
-    def owner(zz):
-        return (((f * 4 + lax.rem(zz, 4)) * NY + iy) * NX + ix) * NC + c, zz // 4
-
-    def giver(zz):
-        return ((zz * NY + iy) * NX + ix) * NC + c, iz // 4
-
-    at_home = iz // 4 == f
-    mine = f * 4 + lax.rem(iz, 4)
-    greeted += [owner(zz) for zz in zpeers]
-    greeted += [giver(lax.rem(mine + d, NZ)) for d in range(1, NZ)]
+    greeted += [node(zz, ypeer, ix, c) for zz in [iz] + zpeers]
+
     barrier = pltpu.get_barrier_semaphore()
     for device in greeted:
         pl.semaphore_signal(barrier, inc=1, device_id=device, device_id_type=MESH)
 
-    @pl.when(jnp.logical_not(at_home))
+    @pl.when(ix == 0)
     def _():
-        pl.semaphore_signal(barrier, inc=1, device_id=owner(iz), device_id_type=MESH)
-        pl.semaphore_signal(barrier, inc=1, device_id=giver(mine), device_id_type=MESH)
+        pl.semaphore_signal(
+            barrier, inc=1, device_id=(near(-2)[0], nf), device_id_type=MESH
+        )
+
+    @pl.when(ix == NX - 1)
+    def _():
+        pl.semaphore_signal(barrier, inc=1, device_id=(near(2)[0], nf), device_id_type=MESH)
 
     loads = []
     for i, (src, dst) in enumerate(
@@ -181,7 +184,7 @@
         made.start()
         loads.append(made)
     loads[0].wait()
-    pl.semaphore_wait(barrier, len(greeted) + 2 * lax.rem(iz // 4 + f, 2))
+    pl.semaphore_wait(barrier, len(greeted) + edge.astype(jnp.int32))
 
     sems = Sems(ssem, rsem)
     step_of = (0, 4, 3 - 2 * c, 1 + 2 * c)
@@ -234,9 +237,6 @@
 
     loop(5, densify)
     loads[2].wait()
-    loads[4].wait()
-    half = pl.ds(pl.multiple_of(c * (N // 2), N // 2), N // 2)
-    wqcopy = sems.copy(wout.at[nf, half, :], wq.at[half, :], across)
 
     def own_s(i):
         sacc[span(i, SUB), :] = dot(a[2, span(i, SUB), :], x[...])
@@ -305,8 +305,12 @@
     if PWHEN == 1:
         send_products()
 
-    wqcopy.wait_recv()
-    wqpass = sems.copy(wq.at[half, :], wq.at[half, :], partner)
+    loads[4].wait()
+    half = pl.ds(pl.multiple_of(c * (N // 2), N // 2), N // 2)
+    wqcopy = [
+        sems.copy(wout.at[nf, half, :], wq.at[0, half, :], across),
+        sems.copy(wout.at[f, half, :], wq.at[1, half, :], across),
+    ]
     loads[3].wait()
 
     def pre_own(k):
@@ -327,6 +331,25 @@
     scopies[-1].wait_recv()
     if PWHEN == 2:
         send_products()
+    hcopies = []
+
+    def hidden_piece(j):
+
+        def act(k):
+            rs = pl.ds(pl.multiple_of(j * RW + k * TILE, TILE), TILE)
+            v = pre[rs, :] + dot(sfull[nf, rs, cs], win[nf, cs, :])
+            g = 1.0 / (1.0 + jnp.exp(-v))
+            hfull[f, rs, :] = (v * g).astype(BF)
+            dact[rs, :] = g * (1.0 + v * (1.0 - g))
+
+        loop(RW // TILE, act)
+        rs = pl.ds(j * RW, RW)
+        hcopies.append(sems.copy(hfull.at[f, rs, :], hfull.at[f, rs, :], peer))
+
+    hidden_piece(0)
+    hidden_piece(1)
+    hidden_piece(2)
+    hidden_piece(3)
     for copy in pcopies:
         copy.wait_recv()
 
@@ -341,189 +364,209 @@
 
     ccopy = sems.copy(cfull.at[f], cfull.at[f], peer)
 
-    hcopies = []
-    for j in range(RCH):
-
-        def act(k, j=j):
-            rs = pl.ds(pl.multiple_of(j * RW + k * TILE, TILE), TILE)
-            v = pre[rs, :] + dot(sfull[nf, rs, cs], win[nf, cs, :])
-            g = 1.0 / (1.0 + jnp.exp(-v))
-            hfull[f, rs, :] = (v * g).astype(BF)
-            dact[rs, :] = g * (1.0 + v * (1.0 - g))
-
-        loop(RW // TILE, act)
-        rs = pl.ds(j * RW, RW)
-        hcopies.append(sems.copy(hfull.at[f, rs, :], hfull.at[f, rs, :], peer))
-
     def z_own(k):
         rs = span(k, SUB)
         zacc[rs, :] = dot(hfull[f, rs, :], wout[f])
 
     loop(N // SUB, z_own)
+    wqpass = []
+    for i in range(2):
+        wqcopy[i].wait_recv()
+        wqpass.append(sems.copy(wq.at[i, half, :], wq.at[i, half, :], partner))
+
+
+    def gout_rows(side):
+        def rows_of(k):
+            part = dot_tn(hfull[side, :, span(k, TILE)], cfull[f])
+            g1[side * 4 + k] = part.reshape(NY, NX, NC, 8, W)
+
+        loop(4, rows_of)
+
+    def side_of(ref, side, *rest):
+        return ref.at[(pl.ds(side * 4, 4), *rest)]
+
+    def to_partner(g, gc, side):
+        return sems.copy(
+            side_of(g, side, slice(None), slice(None), nc), side_of(gc, side), partner
+        )
+
+    def across_x(copy, g, gc, r1, gx, side):
+        copy.wait_recv()
+
+        def first(k):
+            i = side * 4 + k
+            r1[i] = fold(g[i, :, :, c] + gc[i]).astype(BF)
+
+        loop(4, first)
+        return [
+            sems.copy(
+                side_of(r1, side, slice(None), xx), gx.at[d, pl.ds(side * 4, 4)],
+                node(iz, iy, xx, c),
+            )
+            for d, xx in enumerate(xpeers)
+        ]
+
+    gout_rows(f)
+    g1core = [to_partner(g1, g1c, f)]
+
     def bh_own(k):
         rs = span(k, SUB)
         cacc[rs, :] = dot_nt(cfull[f, rs, :], wout[f])
 
     loop(N // SUB, bh_own)
-
-    def gout_cols(side):
-        def rows_of(k):
-            part = dot_tn(hfull[f, :, span(k, TILE)], cfull[side])
-            g1[side * 4 + k] = part.reshape(NY, NX, NC, 8, W)
-
-        loop(4, rows_of)
-
-    gout_cols(f)
-    ccopy.wait_recv()
-    wqpass.wait_recv()
-
-    def close_bp(k):
-        rs = span(k, TILE)
-        back = cacc[rs, :] + dot_nt(cfull[nf, rs, :], wq[...])
-        bp[rs, :] = (back * dact[rs, :]).astype(BF)
-
-    loop(N // TILE, close_bp)
-
-    def gin_rows(k):
-        part = dot_tn(sfull[k // 4, :, span(lax.rem(k, 4), TILE)], bp[...])
-        g2[k] = part.reshape(NY, NX, NC, 8, W)
-
-    loop(NZ, gin_rows)
-    g2core = sems.copy(g2.at[:, :, :, nc], g2c, partner)
-    gout_cols(nf)
-    g1core = sems.copy(g1.at[:, :, :, nc], g1c, partner)
-
-    g2core.wait_recv()
-
-    def g2_first(k):
-        g2r1[k] = fold(g2[k, :, :, c] + g2c[k]).astype(BF)
-
-    loop(NZ, g2_first)
-    g2zc = [
-        sems.copy(g2r1.at[zz], g2z.at[d], node(zz, iy, ix, c)) for d, zz in enumerate(zpeers)
-    ]
-
-    g1core.wait_recv()
-
-    def g1_first(k):
-        g1r1[k] = fold(g1[k, :, :, c] + g1c[k]).astype(BF)
-
-    loop(NZ, g1_first)
-    g1xc = [
-        sems.copy(g1r1.at[:, :, xx], g1x.at[d], node(iz, iy, xx, c))
-        for d, xx in enumerate(xpeers)
-    ]
-
+    for copy in wqpass:
+        copy.wait_recv()
+    g1xc = across_x(g1core[0], g1, g1c, g1r1, g1x, f)
     zcopies = []
-    for j in range(RCH):
+
+    def z_piece(j):
         hcopies[j].wait_recv()
         rs = pl.ds(j * RW, RW)
         z[rs, :] = (zacc[rs, :] + dot(hfull[nf, rs, :], wout[nf])).astype(BF)
-        zcopies.append(spread(z.at[rs, :], lambda i, rs=rs: zg.at[i, rs, :]))
-
+
+        @pl.when(edge)
+        def _():
+            z2[rs, :] = (
+                dot(hfull[f, rs, :], wq[0]) + dot(hfull[nf, rs, :], wq[1])
+            ).astype(BF)
+
+        mine, turned = z.at[rs, :], z2.at[rs, :]
+        zcopies.append([
+            sems.choose(ix != NX - 1, mine, turned, zg.at[0, rs, :], near(2), (near(2)[0], nf)),
+            sems.choose(ix != 0, mine, turned, zg.at[1, rs, :], near(-2), (near(-2)[0], nf)),
+            sems.copy(mine, zg.at[2, rs, :], partner),
+        ])
+
+    z_piece(0)
+    z_piece(1)
+    z_piece(2)
+    z_piece(3)
+    gout_rows(nf)
+    g1core.append(to_partner(g1, g1c, nf))
     def own_o(k):
         rs = span(k, SUB)
         oacc[rs, :] = dot(a[2, rs, :], z[...])
 
     loop(N // SUB, own_o)
-
-    for copy in g1xc:
-        copy.wait_recv()
-
-    def g1_second(k):
-        total = fold(g1[k, :, ix, c] + g1c[k, :, ix])
-        for d in range(NX - 1):
-            total += g1x[d, k].astype(F32)
-        g1r2f[k] = total
-        g1r2[k] = total.astype(BF)
-
-    loop(NZ, g1_second)
-    g1yc = sems.copy(g1r2.at[:, ypeer], g1y, node(iz, ypeer, ix, c))
-
-    for copy in g2zc:
-        copy.wait_recv()
-    total = fold(g2[iz, :, :, c] + g2c[iz])
-    for d in range(NZ - 1):
-        total += g2z[d].astype(F32)
-    g2r2f[...] = total
-    g2r2[...] = total.astype(BF)
-    g2xc = [
-        sems.copy(g2r2.at[:, xx], g2x.at[d], node(iz, iy, xx, c)) for d, xx in enumerate(xpeers)
-    ]
-
-    g1yc.wait_recv()
-    total = g1r2f[:, iy] + g1y[...].astype(F32)
-    g1r3[...] = total.astype(BF)
-    g1zc = [
-        sems.copy(g1r3.at[zz], g1z.at[d + 1], owner(zz)) for d, zz in enumerate(zpeers)
-    ]
-    g1last = sems.make(g1r3.at[iz], g1z.at[0], owner(iz))
-
-    @pl.when(at_home)
-    def _():
-        g1z[0] = g1r3[iz]
-
-    pl.when(jnp.logical_not(at_home))(lambda: g1last.start())
-
-    for copy in g2xc:
-        copy.wait_recv()
-    total = g2r2f[:, ix]
-    for d in range(NX - 1):
-        total += g2x[d].astype(F32)
-    g2r3f[...] = total
-    g2r3[...] = total.astype(BF)
-    g2yc = sems.copy(g2r3.at[ypeer], g2y, node(iz, ypeer, ix, c))
-
-    for j in range(RCH):
-        ks = pl.ds(j * RW, RW)
-        on_side(zcopies[j], nc)
-        relays.append(sems.copy(zg.at[nc, ks, :], zg.at[3, ks, :], partner))
-        zcopies[j][2].wait_recv()
-        on_side(zcopies[j], c)
-
-    def out_add(k):
+    g1xc += across_x(g1core[1], g1, g1c, g1r1, g1x, nf)
+
+    def second(g, gc, gx, r2f, r2):
+        def part(k):
+            total = fold(g[k, :, ix, c] + gc[k, :, ix])
+            for d in range(NX - 1):
+                total += gx[d, k].astype(F32)
+            r2f[k] = total
+            r2[k] = total.astype(BF)
+
+        loop(NZ, part)
+
+    stores = []
+
+    def relay_part(part):
+        made = []
+        for j in range(part * RCH // 2, (part + 1) * RCH // 2):
+            ks = pl.ds(j * RW, RW)
+            on_side(zcopies[j], nc)
+            made.append(sems.copy(zg.at[nc, ks, :], zg.at[3, ks, :], partner))
+            zcopies[j][2].wait_recv()
+            on_side(zcopies[j], c)
+        relays.extend(made)
+        return made
+
+    def out_part(made, part):
+        ks = pl.ds(part * (N // 2), N // 2)
+
+        def direct(k):
+            rs = span(k, SUB)
+            total = oacc[rs, :]
+            for i in range(3):
+                total += dot(a[step_of[i], rs, ks], zg[i, ks, :])
+            oacc[rs, :] = total
+
+        loop(N // SUB, direct)
+        for copy in made:
+            copy.wait_recv()
+        for k in range(N // SUB):
+            rs = pl.ds(k * SUB, SUB)
+            total = oacc[rs, :] + dot(a[step_of[3], rs, ks], zg[3, ks, :])
+            if part == 0:
+                oacc[rs, :] = total
+            else:
+                out_o[rs, :] = total.astype(BF)
+                stores.append(
+                    pltpu.make_async_copy(out_o.at[rs, :], out_h.at[rs, :], lsem.at[10 + k])
+                )
+                stores[-1].start()
+
+
+    far = [
+        (zz, yy) for zz in [iz] + zpeers for yy in (iy, ypeer)
+    ][1:]
+
+    def second(copies, g, gc, gx, r2f, r2, gl):
+        for copy in copies:
+            copy.wait_recv()
+
+        def part(k):
+            total = fold(g[k, :, ix, c] + gc[k, :, ix])
+            for d in range(NX - 1):
+                total += gx[d, k].astype(F32)
+            r2f[k] = total
+            r2[k] = total.astype(BF)
+
+        loop(NZ, part)
+        return [
+            sems.copy(r2.at[zz, yy], gl.at[d], node(zz, yy, ix, c))
+            for d, (zz, yy) in enumerate(far)
+        ]
+
+    def last(copies, r2f, gl, to, into, i):
+        for copy in copies:
+            copy.wait_recv()
+        total = r2f[iz, iy]
+        for d in range(len(far)):
+            total += gl[d].astype(F32)
+        to[:, : W // 2] = total[:8]
+        to[:, W // 2 :] = total[8:]
+        stores.append(pltpu.make_async_copy(to, into, lsem.at[i]))
+        stores[-1].start()
+
+    part0 = relay_part(0)
+    out_part(part0, 0)
+    g1last = second(g1xc, g1, g1c, g1x, g1r2f, g1r2, g1l)
+    ccopy.wait_recv()
+
+    def close_bp(k):
         rs = span(k, SUB)
-        total = oacc[rs, :]
-        for i in range(3):
-            total += dot(a[step_of[i], rs, :], zg[i])
-        oacc[rs, :] = total
-
-    loop(N // SUB, out_add)
-    for relay in relays[XCH:]:
-        relay.wait_recv()
-
-    stores = []
-    for k in range(N // SUB):
-        rs = pl.ds(k * SUB, SUB)
-        out_o[rs, :] = (oacc[rs, :] + dot(a[step_of[3], rs, :], zg[3])).astype(BF)
-        stores.append(pltpu.make_async_copy(out_o.at[rs, :], out_h.at[rs, :], lsem.at[10 + k]))
-        stores[-1].start()
-
-    g2yc.wait_recv()
-    total = g2r3f[iy] + g2y[...].astype(F32)
-    gin_o[:, : W // 2] = total[:8]
-    gin_o[:, W // 2 :] = total[8:]
-    stores.append(pltpu.make_async_copy(gin_o, gin_h, lsem.at[8]))
-    stores[-1].start()
-
-    for copy in g1zc:
-        copy.wait_recv()
-    pl.when(jnp.logical_not(at_home))(lambda: g1last.wait_recv())
-    total = g1z[0].astype(F32)
-    for d in range(1, NZ):
-        total += g1z[d].astype(F32)
-    gout_o[:, : W // 2] = total[:8]
-    gout_o[:, W // 2 :] = total[8:]
-    stores.append(pltpu.make_async_copy(gout_o, gout_h, lsem.at[9]))
-    stores[-1].start()
+        back = cacc[rs, :] + dot_nt(cfull[nf, rs, :], wq[0])
+        bp[rs, :] = (back * dact[rs, :]).astype(BF)
+
+    loop(N // SUB, close_bp)
+    g2core = []
+    for side in range(2):
+
+        def gin_rows(k, side=side):
+            part = dot_tn(sfull[side, :, span(k, TILE)], bp[...])
+            g2[side * 4 + k] = part.reshape(NY, NX, NC, 8, W)
+
+        loop(4, gin_rows)
+        g2core.append(to_partner(g2, g2c, side))
+    g2xc = []
+    for side in range(2):
+        g2xc += across_x(g2core[side], g2, g2c, g2r1, g2x, side)
+    part1 = relay_part(1)
+    out_part(part1, 1)
+    last(g1last, g1r2f, g1l, gout_o, gout_h, 9)
+    g2last = second(g2xc, g2, g2c, g2x, g2r2f, g2r2, g2l)
+    last(g2last, g2r2f, g2l, gin_o, gin_h, 8)
 
     sent = [copy for group in xcopies + zcopies for copy in group] + pcopies + scopies + hcopies + relays
-    sent += [help_copy, wqcopy, wqpass, ccopy, g2core, g1core, g1yc, g2yc] + g2zc + g1xc + g2xc + g1zc
+    sent += [help_copy, ccopy] + g2core + g1core + wqcopy + wqpass
+    sent += g1xc + g2xc + g1last + g2last
     for copy in stores:
         copy.wait()
     for copy in sent:
         copy.wait_send()
-    pl.when(jnp.logical_not(at_home))(lambda: g1last.wait_send())
 
 
 def hand_over(a_ref, b_ref, c_ref, a_o, b_o, c_o, a_v, b_v, c_v, insem, outsem):
@@ -550,17 +593,15 @@
         V((N, W), BF), V((8, W), F32), V((8, W), F32),
         V((N, W), BF), V((2, 512, W), BF), V((2, 512, W), BF), V((5, 8, TILE, TILE), BF), V((N, W), BF),
         V((5, N, N), BF), V((4, N, W), BF), V((N, W), F32), V((2, N, W), BF), V((N, W), F32),
-        V((2, N, W), BF), V((N, W), F32), V((N, W), F32), V((N, W), BF), V((4, N, W), BF),
-        V((4, N, W), BF), V((4, N, W), BF), V((N, W), F32), V((2, N, W), BF), V((N, W), BF),
+        V((2, N, W), BF), V((N, W), F32), V((N, W), F32), V((N, W), BF), V((N, W), BF), V((4, N, W), BF),
+        V((4, N, W), BF), V((4, N, W), BF), V((N, W), F32), V((2, N, W), BF), V((2, N, W), BF),
         V((N, W), BF), V((N, W), F32), V((N - N * SPLIT // 4, W), BF),
         V((NZ, NY, NX, NC, 8, W), F32), V((NZ, NY, NX, 8, W), F32), V((NZ, NY, NX, 16, W // 2), BF),
         V((3, NZ, NY, 16, W // 2), BF), V((NZ, NY, 16, W // 2), F32), V((NZ, NY, 16, W // 2), BF),
-        V((NZ, 16, W // 2), BF), V((NZ, 16, W // 2), BF),
-        V((NZ, 16, W // 2), BF),
+        V((15, 16, W // 2), BF),
         V((NZ, NY, NX, NC, 8, W), F32), V((NZ, NY, NX, 8, W), F32), V((NZ, NY, NX, 16, W // 2), BF),
-        V((7, NY, NX, 16, W // 2), BF), V((NY, NX, 16, W // 2), F32), V((NY, NX, 16, W // 2), BF),
-        V((3, NY, 16, W // 2), BF), V((NY, 16, W // 2), F32), V((NY, 16, W // 2), BF),
-        V((16, W // 2), BF),
+        V((3, NZ, NY, 16, W // 2), BF), V((NZ, NY, 16, W // 2), F32), V((NZ, NY, 16, W // 2), BF),
+        V((15, 16, W // 2), BF),
         pltpu.SemaphoreType.DMA((8 + 2 + N // SUB,)),
         pltpu.SemaphoreType.DMA((NREMOTE,)),
         pltpu.SemaphoreType.DMA((NREMOTE,)),

time: 99.5 us -> 95.4 us (0.959)
  Pallas kernels: 98.7 us -> 94.2 us
    pallas_call x1, Pallas kernels: 96.8 us -> 92.3 us  [shards(): pl.pallas_call(kernel, out_shape=(jax.ShapeDtypeStruct((N, W), BF), jax.S...]
where the time goes in v5:
time: 95.4 us; the launch traced here: 94.9 us
  Pallas kernels  94.2 us (99%)
    pallas_call x1, Pallas kernels, shards(): pl.pallas_call(kernel, out_shape=(jax.ShapeDtypeStruct((N, W), BF), jax.S...  92.3 us

profile of v5, /device:TPU:1, one launch (start us, length us, event | category | flops | bytes accessed | tf_op | source)
XLA Modules:
  0.0 94.9 jit_solution(10327812189916890202)
XLA Ops:
  0.6 92.3 %graph_layers.1 = (bf16[512,512]{1,0:T(8,128)(2,1)}, f32[8,512]{1,0:T(8,128)}, f32[8,512]{1,0:T(8,128)}) custom-call(bf16[512,512]{1,0:T(8,128)(2,1)} %x_h.1, bf16[2,512,512]{2,1,0:T(8,128)(2,1)} %bitcast.6, bf16[2,512,512]{2,1,0:T(8,128)(2,1)} %bitcast.7, bf16[5,8,128,128]{3,2,1,0:T(8,128)(2,1)} %bitcast.5, s32[5,1,8]{2,1,0:T(1,128)} %bitcast.8, ...), custom_call_target="tpu_custom_call" | custom-call | tf_op jit(solution)/shard_map/graph_layers/pallas_call | solution.py:609
  93.0 1.9 %hand_over.1 = (bf16[512,512]{1,0:T(8,128)(2,1)}, f32[8,512]{1,0:T(8,128)}, f32[8,512]{1,0:T(8,128)}) custom-call(bf16[512,512]{1,0:T(8,128)(2,1)} %get-tuple-element.6.a_ref, f32[8,512]{1,0:T(8,128)} %get-tuple-element.7.b_ref, f32[8,512]{1,0:T(8,128)} %get-tuple-element.8.c_ref), custom_call_target="tpu_custom_call" | custom-call | tf_op jit(solution)/shard_map/hand_over/pallas_call | solution.py:633

commit v6 on v5

--- a/solution.py
+++ b/solution.py
@@ -19,7 +19,8 @@
 XW = W // XCH
 RCH = 4
 PWHEN = 0
-SPLIT = 3
+SPLIT = 5
+CSPLIT = 6
 RW = N // RCH
 SUB = 256
 
@@ -102,7 +103,6 @@
             self.on.start()
 
     def wait_recv(self):
-        self.pass_on()
         self.lo.wait_recv()
         self.pick(self.on.wait_recv, self.straight.wait_recv)
 
@@ -125,7 +125,7 @@
     rows, cols, cnts, out_o, gin_o, gout_o,
     x, win, wout, tiles, cot,
     a, xg, sacc, sfull, pre, hfull, dact, zacc, z, z2, zg,
-    pbuf, pr, cacc, cfull, wq, bp, oacc, sway,
+    pbuf, pr, cacc, cfull, wq, bp, oacc, sway, cway,
     g1, g1c, g1r1, g1x, g1r2f, g1r2, g1l,
     g2, g2c, g2r1, g2x, g2r2f, g2r2, g2l,
     lsem, ssem, rsem,
@@ -189,8 +189,8 @@
     sems = Sems(ssem, rsem)
     step_of = (0, 4, 3 - 2 * c, 1 + 2 * c)
 
-    def swap(ref, out_slot, in_slot, start, size, cs, way):
-        near_rows = size * SPLIT // 4
+    def swap(ref, out_slot, in_slot, start, size, cs, way, split):
+        near_rows = size * split // 8
         lo, hi = pl.ds(start, near_rows), pl.ds(start + near_rows, size - near_rows)
         return Swap(
             sems, edge,
@@ -300,7 +300,7 @@
         relay.wait_recv()
         add(3, True)
         scopies.append(
-            swap(lambda i, r, q: sfull.at[i, r, q], f, (f, nf), 0, N, cs, sway.at[:, cs])
+            swap(lambda i, r, q: sfull.at[i, r, q], f, (f, nf), 0, N, cs, sway.at[:, cs], SPLIT)
         )
     if PWHEN == 1:
         send_products()
@@ -320,6 +320,7 @@
     loop(N // SUB, pre_own)
     for j in range(XCH - 1):
         cs = pl.ds(j * XW, XW)
+        scopies[j].pass_on()
         scopies[j].wait_recv()
 
         def pre_add(k):
@@ -328,6 +329,7 @@
 
         loop(N // SUB, pre_add)
     cs = pl.ds((XCH - 1) * XW, XW)
+    scopies[-1].pass_on()
     scopies[-1].wait_recv()
     if PWHEN == 2:
         send_products()
@@ -362,7 +364,9 @@
 
     loop(N // TILE, close_c)
 
-    ccopy = sems.copy(cfull.at[f], cfull.at[f], peer)
+    ccopy = swap(
+        lambda i, r, q: cfull.at[i, r, q], f, (f, nf), 0, N, pl.ds(0, W), cway, CSPLIT
+    )
 
     def z_own(k):
         rs = span(k, SUB)
@@ -531,9 +535,9 @@
         stores.append(pltpu.make_async_copy(to, into, lsem.at[i]))
         stores[-1].start()
 
+    ccopy.pass_on()
     part0 = relay_part(0)
     out_part(part0, 0)
-    g1last = second(g1xc, g1, g1c, g1x, g1r2f, g1r2, g1l)
     ccopy.wait_recv()
 
     def close_bp(k):
@@ -554,10 +558,11 @@
     g2xc = []
     for side in range(2):
         g2xc += across_x(g2core[side], g2, g2c, g2r1, g2x, side)
+    g1last = second(g1xc, g1, g1c, g1x, g1r2f, g1r2, g1l)
     part1 = relay_part(1)
     out_part(part1, 1)
+    g2last = second(g2xc, g2, g2c, g2x, g2r2f, g2r2, g2l)
     last(g1last, g1r2f, g1l, gout_o, gout_h, 9)
-    g2last = second(g2xc, g2, g2c, g2x, g2r2f, g2r2, g2l)
     last(g2last, g2r2f, g2l, gin_o, gin_h, 8)
 
     sent = [copy for group in xcopies + zcopies for copy in group] + pcopies + scopies + hcopies + relays
@@ -595,7 +600,7 @@
         V((5, N, N), BF), V((4, N, W), BF), V((N, W), F32), V((2, N, W), BF), V((N, W), F32),
         V((2, N, W), BF), V((N, W), F32), V((N, W), F32), V((N, W), BF), V((N, W), BF), V((4, N, W), BF),
         V((4, N, W), BF), V((4, N, W), BF), V((N, W), F32), V((2, N, W), BF), V((2, N, W), BF),
-        V((N, W), BF), V((N, W), F32), V((N - N * SPLIT // 4, W), BF),
+        V((N, W), BF), V((N, W), F32), V((N - N * SPLIT // 8, W), BF), V((N - N * CSPLIT // 8, W), BF),
         V((NZ, NY, NX, NC, 8, W), F32), V((NZ, NY, NX, 8, W), F32), V((NZ, NY, NX, 16, W // 2), BF),
         V((3, NZ, NY, 16, W // 2), BF), V((NZ, NY, 16, W // 2), F32), V((NZ, NY, 16, W // 2), BF),
         V((15, 16, W // 2), BF),

time: 95.4 us -> 89 us (0.933)
  Pallas kernels: 94.2 us -> 88.2 us
    pallas_call x1, Pallas kernels: 92.3 us -> 86.3 us  [shards(): pl.pallas_call(kernel, out_shape=(jax.ShapeDtypeStruct((N, W), BF), jax.S...]
where the time goes in v6:
time: 89 us; the launch traced here: 88.8 us
  Pallas kernels  88.2 us (99%)
    pallas_call x1, Pallas kernels, shards(): pl.pallas_call(kernel, out_shape=(jax.ShapeDtypeStruct((N, W), BF), jax.S...  86.3 us
    pallas_call x1, Pallas kernels, shards(): pl.pallas_call(hand_over, out_shape=tuple((jax.ShapeDtypeStruct(r.shape,...  1.89 us

profile of v6, /device:TPU:1, one launch (start us, length us, event | category | flops | bytes accessed | tf_op | source)
XLA Modules:
  0.0 88.8 jit_solution(3803784242604929037)
XLA Ops:
  0.6 86.3 %graph_layers.1 = (bf16[512,512]{1,0:T(8,128)(2,1)}, f32[8,512]{1,0:T(8,128)}, f32[8,512]{1,0:T(8,128)}) custom-call(bf16[512,512]{1,0:T(8,128)(2,1)} %x_h.1, bf16[2,512,512]{2,1,0:T(8,128)(2,1)} %bitcast.6, bf16[2,512,512]{2,1,0:T(8,128)(2,1)} %bitcast.7, bf16[5,8,128,128]{3,2,1,0:T(8,128)(2,1)} %bitcast.5, s32[5,1,8]{2,1,0:T(1,128)} %bitcast.8, ...), custom_call_target="tpu_custom_call" | custom-call | tf_op jit(solution)/shard_map/graph_layers/pallas_call | solution.py:614
  86.9 1.9 %hand_over.1 = (bf16[512,512]{1,0:T(8,128)(2,1)}, f32[8,512]{1,0:T(8,128)}, f32[8,512]{1,0:T(8,128)}) custom-call(bf16[512,512]{1,0:T(8,128)(2,1)} %get-tuple-element.6.a_ref, f32[8,512]{1,0:T(8,128)} %get-tuple-element.7.b_ref, f32[8,512]{1,0:T(8,128)} %get-tuple-element.8.c_ref), custom_call_target="tpu_custom_call" | custom-call | tf_op jit(solution)/shard_map/hand_over/pallas_call | solution.py:638

commit v7 on v6

--- a/solution.py
+++ b/solution.py
@@ -152,8 +152,8 @@
     turn, onward = (beside_node, nf), (beside_node, f)
     across = (((iz * NY + 1 - iy) * NX + ix) * NC + c, nf)
     partner = node(iz, iy, ix, nc)
-    xpeers = [lax.rem(ix + d, NX) for d in range(1, NX)]
-    zpeers = [lax.rem(iz + d, NZ) for d in range(1, NZ)]
+    xpeers = [lax.rem(ix + d, NX) for d in (2, 1, 3)]
+    zpeers = [lax.rem(iz + d, NZ) for d in (4, 3, 5, 2, 6, 1, 7)]
     ypeer = 1 - iy
 
     greeted = [near(2), near(-2), peer, partner, turn, across]
@@ -453,6 +453,57 @@
 
     loop(N // SUB, own_o)
     g1xc += across_x(g1core[1], g1, g1c, g1r1, g1x, nf)
+
+    def second(g, gc, gx, r2f, r2):
+        def part(k):
+            total = fold(g[k, :, ix, c] + gc[k, :, ix])
+            for d in range(NX - 1):
+                total += gx[d, k].astype(F32)
+            r2f[k] = total
+            r2[k] = total.astype(BF)
+
+        loop(NZ, part)
+
+    stores = []
+
+    def relay_part(part):
+        made = []
+        for j in range(part * RCH // 2, (part + 1) * RCH // 2):
+            ks = pl.ds(j * RW, RW)
+            on_side(zcopies[j], nc)
+            made.append(sems.copy(zg.at[nc, ks, :], zg.at[3, ks, :], partner))
+            zcopies[j][2].wait_recv()
+            on_side(zcopies[j], c)
+        relays.extend(made)
+        return made
+
+    def out_part(made, part):
+        ks = pl.ds(part * (N // 2), N // 2)
+
+        def direct(k):
+            rs = span(k, SUB)
+            total = oacc[rs, :]
+            for i in range(3):
+                total += dot(a[step_of[i], rs, ks], zg[i, ks, :])
+            oacc[rs, :] = total
+
+        loop(N // SUB, direct)
+        for copy in made:
+            copy.wait_recv()
+        for k in range(N // SUB):
+            rs = pl.ds(k * SUB, SUB)
+            total = oacc[rs, :] + dot(a[step_of[3], rs, ks], zg[3, ks, :])
+            if part == 0:
+                oacc[rs, :] = total
+            else:
+                out_o[rs, :] = total.astype(BF)
+                stores.append(
+                    pltpu.make_async_copy(out_o.at[rs, :], out_h.at[rs, :], lsem.at[10 + k])
+                )
+                stores[-1].start()
+
+
+    far = [(zz, yy) for zz in zpeers for yy in (ypeer, iy)] + [(iz, ypeer)]
 
     def second(g, gc, gx, r2f, r2):
         def part(k):

time: 89 us -> 88.5 us (level)
  no operation moved by 1% of the time
where the time goes in v7:
time: 88.5 us; the launch traced here: 88 us
  Pallas kernels  87.4 us (99%)
    pallas_call x1, Pallas kernels, shards(): pl.pallas_call(kernel, out_shape=(jax.ShapeDtypeStruct((N, W), BF), jax.S...  85.5 us
    pallas_call x1, Pallas kernels, shards(): pl.pallas_call(hand_over, out_shape=tuple((jax.ShapeDtypeStruct(r.shape,...  1.89 us

profile of v7, /device:TPU:1, one launch (start us, length us, event | category | flops | bytes accessed | tf_op | source)
XLA Modules:
  0.0 88.0 jit_solution(4468020458639238717)
XLA Ops:
  0.6 85.5 %graph_layers.1 = (bf16[512,512]{1,0:T(8,128)(2,1)}, f32[8,512]{1,0:T(8,128)}, f32[8,512]{1,0:T(8,128)}) custom-call(bf16[512,512]{1,0:T(8,128)(2,1)} %x_h.1, bf16[2,512,512]{2,1,0:T(8,128)(2,1)} %bitcast.6, bf16[2,512,512]{2,1,0:T(8,128)(2,1)} %bitcast.7, bf16[5,8,128,128]{3,2,1,0:T(8,128)(2,1)} %bitcast.5, s32[5,1,8]{2,1,0:T(1,128)} %bitcast.8, ...), custom_call_target="tpu_custom_call" | custom-call | tf_op jit(solution)/shard_map/graph_layers/pallas_call | solution.py:665
  86.2 1.9 %hand_over.1 = (bf16[512,512]{1,0:T(8,128)(2,1)}, f32[8,512]{1,0:T(8,128)}, f32[8,512]{1,0:T(8,128)}) custom-call(bf16[512,512]{1,0:T(8,128)(2,1)} %get-tuple-element.6.a_ref, f32[8,512]{1,0:T(8,128)} %get-tuple-element.7.b_ref, f32[8,512]{1,0:T(8,128)} %get-tuple-element.8.c_ref), custom_call_target="tpu_custom_call" | custom-call | tf_op jit(solution)/shard_map/hand_over/pallas_call | solution.py:689
